TPU v7x, 32 devices: a whole 2x2x4 slice. The times are simulated.
32 devices in a mesh: dp: 8 (over y, x, core), tensor: 4 (over z).
Axes of the slice: x: 2, y: 2, z: 4, core: 2. Of those that a mesh axis runs over, the one named last changes fastest.
Arguments:
- latents: bfloat16 [16384, 1280], P('dp'), may hold values from -6 to 6
- norm1_gain: float32 [1280], replicated, may hold values from 0.5 to 1.5
- norm1_shift: float32 [1280], replicated, may hold values from -1.75 to 1.75
- query_weight: bfloat16 [1280, 1280], P(None, 'tensor'), may hold values from -0.15625 to 0.15625
- query_bias: float32 [1280], P('tensor'), may hold values from -1.75 to 1.75
- key_weight: bfloat16 [1280, 1280], P(None, 'tensor'), may hold values from -0.15625 to 0.15625
- value_weight: bfloat16 [1280, 1280], P(None, 'tensor'), may hold values from -0.15625 to 0.15625
- value_bias: float32 [1280], P('tensor'), may hold values from -1.75 to 1.75
- out_weight: bfloat16 [1280, 1280], P('tensor'), may hold values from -0.625 to 0.625
- out_bias: float32 [1280], replicated, may hold values from -1.75 to 1.75
- norm2_gain: float32 [1280], replicated, may hold values from 0.5 to 1.5
- norm2_shift: float32 [1280], replicated, may hold values from -1.75 to 1.75
- hidden_weight: bfloat16 [1280, 1280], P(None, 'tensor'), may hold values from -0.15625 to 0.15625
- hidden_bias: float32 [1280], P('tensor'), may hold values from -1.75 to 1.75
- proj_weight: bfloat16 [1280, 1280], P('tensor'), may hold values from -0.25 to 0.25
- proj_bias: float32 [1280], replicated, may hold values from -1.75 to 1.75
- segments: int32 [16, 1024], P('dp'), may hold values from 0 to 7, never falling along the last dimension, each value on 1 to 512 neighbouring positions
- valid_mask: int32 [16, 1024], P('dp'), may hold values 0 or 1
- cotangent: bfloat16 [16384, 1280], P('dp'), may hold values from -6 to 6
Outputs:
- output: bfloat16 [16384, 1280], P('dp')
- grad_input: float32 [16384, 1280], P('dp')
- grad_norm1_gain: float32 [1280], replicated
- grad_norm1_shift: float32 [1280], replicated
- grad_query_weight: float32 [1280, 1280], P(None, 'tensor')
- grad_query_bias: float32 [1280], P('tensor')
- grad_key_weight: float32 [1280, 1280], P(None, 'tensor')
- grad_value_weight: float32 [1280, 1280], P(None, 'tensor')
- grad_value_bias: float32 [1280], P('tensor')
- grad_out_weight: float32 [1280, 1280], P('tensor')
- grad_out_bias: float32 [1280], replicated
- grad_norm2_gain: float32 [1280], replicated
- grad_norm2_shift: float32 [1280], replicated
- grad_hidden_weight: float32 [1280, 1280], P(None, 'tensor')
- grad_hidden_bias: float32 [1280], P('tensor')
- grad_proj_weight: float32 [1280, 1280], P('tensor')
- grad_proj_bias: float32 [1280], replicated
- rms: float32 [16, 3], P('dp')
Inputs may be any that keep to these rules, and one draw needn't show every extreme that they name: `segments`: in each row segment numbers never fall, each document has 1 to 512 positions, and one has exactly that many.
All inputs are finite; a program needn't handle non-finite values. No bound on the sum of `valid_mask` on one device may be relied on, other than what follows from the above.
Results may differ from a plain program's by a relative error of at most 0.013.
Values sent between devices are 32-bit elements; how exact they have to be, the bound alone decides.
A program may use at most 192 MiB of HBM per device.

v0:
```python
import math

import jax
import jax.numpy as jnp
from jax import lax
from jax.sharding import PartitionSpec as P

HEAD_DIM = 160


EPS = 1e-05
NEG = -1e30


def layer_norm(v, gain, shift):
    center = v - jnp.mean(v, axis=-1, keepdims=True)
    spread = jnp.mean(center * center, axis=-1, keepdims=True)
    return center * lax.rsqrt(spread + EPS) * gain + shift


def inner(left, right):
    return lax.dot_general(
        left, right, (((0,), (0,)), ((), ())), preferred_element_type=jnp.float32
    )


def outer(left, right):
    return lax.dot_general(
        left, right, (((1,), (1,)), ((), ())), preferred_element_type=jnp.float32
    )


def mask_of(seg):
    length = seg.shape[0]
    rowpos = lax.broadcasted_iota(jnp.int32, (length, length), 0)
    colpos = lax.broadcasted_iota(jnp.int32, (length, length), 1)
    return ((rowpos >= colpos) & (seg[:, None] == seg[None, :]))[None]


def scores_of(query, keyed, seg):
    scores = jnp.einsum(
        "qhe,khe->hqk", query, keyed, preferred_element_type=jnp.float32
    ) / math.sqrt(HEAD_DIM)
    allowed = mask_of(seg)
    return (jnp.where(allowed, scores, NEG), allowed)


def attend_forward(query, keyed, valued, seg):
    scores, allowed = scores_of(query, keyed, seg)
    top = jnp.max(scores, axis=-1, keepdims=True)
    weights = jnp.where(allowed, jnp.exp(scores - top), 0.0)
    total = jnp.sum(weights, axis=-1, keepdims=True)
    probs = (weights / total).astype(jnp.bfloat16)
    mixed = jnp.einsum("hqk,khe->qhe", probs, valued, preferred_element_type=jnp.float32).astype(
        jnp.bfloat16
    )
    return (mixed, (top + jnp.log(total))[..., 0])


def attend_backward(query, keyed, valued, seg, logsum, d_mixed):
    scores, allowed = scores_of(query, keyed, seg)
    probs = jnp.where(allowed, jnp.exp(scores - logsum[..., None]), 0.0)
    low_probs = probs.astype(jnp.bfloat16)
    d_valued = jnp.einsum(
        "hqk,qhe->khe", low_probs, d_mixed, preferred_element_type=jnp.float32
    ).astype(jnp.bfloat16)
    d_probs = jnp.einsum("qhe,khe->hqk", d_mixed, valued, preferred_element_type=jnp.float32)
    d_scores = probs * (d_probs - jnp.sum(probs * d_probs, axis=-1, keepdims=True))
    low_scores = d_scores.astype(jnp.bfloat16)
    scale = 1.0 / math.sqrt(HEAD_DIM)
    d_query = (
        jnp.einsum("hqk,khe->qhe", low_scores, keyed, preferred_element_type=jnp.float32) * scale
    ).astype(jnp.bfloat16)
    d_keyed = (
        jnp.einsum("hqk,qhe->khe", low_scores, query, preferred_element_type=jnp.float32) * scale
    ).astype(jnp.bfloat16)
    return (d_query, d_keyed, d_valued)


def shards(
    latents,
    norm1_gain,
    norm1_shift,
    query_weight,
    query_bias,
    key_weight,
    value_weight,
    value_bias,
    out_weight,
    out_bias,
    norm2_gain,
    norm2_shift,
    hidden_weight,
    hidden_bias,
    proj_weight,
    proj_bias,
    segments,
    valid_mask,
    cotangent,
):
    seq_count, length = segments.shape
    tok_rows, width = latents.shape
    local_heads = query_weight.shape[1] // HEAD_DIM

    def split(t):
        return t.reshape(seq_count, length, local_heads, HEAD_DIM)

    inputs = latents.astype(jnp.float32)
    normed1 = layer_norm(inputs, norm1_gain, norm1_shift).astype(jnp.bfloat16)
    query = (
        jnp.dot(normed1, query_weight, preferred_element_type=jnp.float32) + query_bias
    ).astype(jnp.bfloat16)
    keyed = jnp.dot(normed1, key_weight, preferred_element_type=jnp.float32).astype(jnp.bfloat16)
    valued = (
        jnp.dot(normed1, value_weight, preferred_element_type=jnp.float32) + value_bias
    ).astype(jnp.bfloat16)
    mixed, logsum = lax.map(
        lambda t: attend_forward(t[0], t[1], t[2], t[3]),
        (split(query), split(keyed), split(valued), segments),
    )
    mixed = mixed.reshape(tok_rows, local_heads * HEAD_DIM)
    attended = (
        lax.psum(jnp.dot(mixed, out_weight, preferred_element_type=jnp.float32), "tensor")
        + out_bias
    )
    resid = inputs + attended
    normed2 = layer_norm(resid, norm2_gain, norm2_shift).astype(jnp.bfloat16)
    pre = jnp.dot(normed2, hidden_weight, preferred_element_type=jnp.float32) + hidden_bias
    act = jax.nn.gelu(pre, approximate=False).astype(jnp.bfloat16)
    branch = (
        lax.psum(jnp.dot(act, proj_weight, preferred_element_type=jnp.float32), "tensor")
        + proj_bias
    )
    output = resid + branch
    weight = valid_mask.astype(jnp.float32)
    counted = jnp.maximum(jnp.sum(weight, axis=1), 1.0) * width

    def per_seq(v):
        return jnp.sum(weight * jnp.sum(v * v, axis=-1).reshape(seq_count, length), axis=1)

    stat_sums = jnp.stack([per_seq(attended), per_seq(branch), per_seq(output)], axis=1)
    rms = jnp.sqrt(stat_sums / counted[:, None])
    grad_out = cotangent.astype(jnp.float32)
    grad_w2 = inner(act, cotangent)
    grad_b2 = jnp.sum(grad_out, axis=0)
    d_act = outer(cotangent, proj_weight)
    d_pre = jax.vjp(lambda t: jax.nn.gelu(t, approximate=False), pre)[1](d_act)[0]
    low_pre = d_pre.astype(jnp.bfloat16)
    grad_w1 = inner(normed2, low_pre)
    grad_b1 = jnp.sum(low_pre.astype(jnp.float32), axis=0)
    d_normed2 = lax.psum(outer(low_pre, hidden_weight), "tensor")
    norm_back2 = jax.vjp(layer_norm, resid, norm2_gain, norm2_shift)[1]
    d_resid_norm, grad_g2, grad_c2 = norm_back2(d_normed2)
    d_resid = grad_out + d_resid_norm
    low_attended = d_resid.astype(jnp.bfloat16)
    grad_bo = jnp.sum(low_attended.astype(jnp.float32), axis=0)
    grad_wo = inner(mixed, low_attended)
    d_mixed = outer(low_attended, out_weight).astype(jnp.bfloat16)
    d_query, d_keyed, d_valued = lax.map(
        lambda t: attend_backward(t[0], t[1], t[2], t[3], t[4], t[5]),
        (split(query), split(keyed), split(valued), segments, logsum, split(d_mixed)),
    )
    d_query = d_query.reshape(tok_rows, local_heads * HEAD_DIM)
    d_keyed = d_keyed.reshape(tok_rows, local_heads * HEAD_DIM)
    d_valued = d_valued.reshape(tok_rows, local_heads * HEAD_DIM)
    grad_wq = inner(normed1, d_query)
    grad_bq = jnp.sum(d_query.astype(jnp.float32), axis=0)
    grad_wk = inner(normed1, d_keyed)
    grad_wv = inner(normed1, d_valued)
    grad_bv = jnp.sum(d_valued.astype(jnp.float32), axis=0)
    partial_in = (
        outer(d_query, query_weight) + outer(d_keyed, key_weight) + outer(d_valued, value_weight)
    )
    d_normed1 = lax.psum(partial_in, "tensor")
    norm_back1 = jax.vjp(layer_norm, inputs, norm1_gain, norm1_shift)[1]
    d_input_norm, grad_g1, grad_c1 = norm_back1(d_normed1)
    grad_input = d_resid + d_input_norm
    (
        grad_g1,
        grad_c1,
        grad_wq,
        grad_bq,
        grad_wk,
        grad_wv,
        grad_bv,
        grad_wo,
        grad_bo,
        grad_g2,
        grad_c2,
        grad_w1,
        grad_b1,
        grad_w2,
        grad_b2,
    ) = lax.psum(
        (
            grad_g1,
            grad_c1,
            grad_wq,
            grad_bq,
            grad_wk,
            grad_wv,
            grad_bv,
            grad_wo,
            grad_bo,
            grad_g2,
            grad_c2,
            grad_w1,
            grad_b1,
            grad_w2,
            grad_b2,
        ),
        "dp",
    )
    return (
        output.astype(jnp.bfloat16),
        grad_input,
        grad_g1,
        grad_c1,
        grad_wq,
        grad_bq,
        grad_wk,
        grad_wv,
        grad_bv,
        grad_wo,
        grad_bo,
        grad_g2,
        grad_c2,
        grad_w1,
        grad_b1,
        grad_w2,
        grad_b2,
        rms,
    )


def solution(mesh):
    placed = (
        P("dp", None),
        P(),
        P(),
        P(None, "tensor"),
        P("tensor"),
        P(None, "tensor"),
        P(None, "tensor"),
        P("tensor"),
        P("tensor", None),
        P(),
        P(),
        P(),
        P(None, "tensor"),
        P("tensor"),
        P("tensor", None),
        P(),
        P("dp", None),
        P("dp", None),
        P("dp", None),
    )
    return jax.shard_map(
        shards,
        mesh=mesh,
        in_specs=placed,
        out_specs=(
            P("dp", None),
            P("dp", None),
            P(),
            P(),
            P(None, "tensor"),
            P("tensor"),
            P(None, "tensor"),
            P(None, "tensor"),
            P("tensor"),
            P("tensor", None),
            P(),
            P(),
            P(),
            P(None, "tensor"),
            P("tensor"),
            P("tensor", None),
            P(),
            P("dp", None),
        ),
        check_vma=False,
    )
```

profile of v0, /device:TPU:0, one launch (start us, length us, event | category | flops | bytes accessed | tf_op | source)
XLA Modules:
  0.0 1821.9 jit_solution(10788580656488504458)
XLA Ops:
  41.4 20.7 %while.26 = (s32[]{:T(128)}, bf16[2,1024,2,160]{1,3,2,0:T(8,128)(2,1)}, f32[2,2,1024]{2,1,0:T(2,128)S(1)}, bf16[2,1024,2,160]{1,3,2,0:T(8,128)(2,1)S(1)}, s32[2,...) while((s32[]{:T(128)}, ...), condition=%wide.region_5.6_spmd, body=%wide.region_2.5_spmd.sunk | while | flops 1375008768 | bytes 42547356 | solution.py:117
  73.1 361.1 %all-reduce.8.cloned.1.call-done = f32[2048,1280]{1,0:T(8,128)} async-done(((f32[2048,1280]{1,0:T(8,128)}), f32[2048,1280]{1,0:T(8,128)}) %all-reduce.8.cloned.1.call-update) | async-done | bytes 10485776 | tf_op jit(solution)/shard_map/psum | solution.py:123
  434.2 11.8 fusion.86
  459.2 10.2 convert_reduce_fusion.3
  481.3 697.5 %all-reduce.14.cloned.1.call-done = (f32[2048,1280]{1,0:T(8,128)}, f32[2048,1280]{1,0:T(8,128)}) async-done(((f32[2048,1280]{1,0:T(8,128)}, f32[2048,1280]{1,0:T(8,128)}), (f32[2048,1280]{1,0:T(8,128)}, f32[2048,1280]{1,0:T(8,128)})) %all-reduce.14.cloned.1.call-update) | async-done | bytes 20971536 | tf_op jit(solution)/shard_map/psum | solution.py:131
  1178.8 15.7 multiply_reduce_fusion.2
  1200.7 7.7 convert_reduce_fusion.2
  1219.9 55.4 %while.27 = (s32[]{:T(128)}, bf16[2,1024,2,160]{1,3,2,0:T(8,128)(2,1)}, bf16[2,1024,2,160]{1,3,2,0:T(8,128)(2,1)}, bf16[2,1024,2,160]{1,3,2,0:T(8,128)(2,1)}, bf...) while((s32[]{:T(128)}, ...), condition=%wide.region_15.16_spmd, body=%wide.region_13.15_spmd.sunk | while | flops 3381196800 | bytes 147121552 | solution.py:159
  1223.6 6.0 multiply_reduce_fusion.11
  1229.7 8.2 multiply_convert_fusion.3
  1237.9 6.0 fusion.171
  1251.0 6.0 multiply_reduce_fusion.11
  1257.1 8.2 multiply_convert_fusion.3
  1265.3 6.0 fusion.171
  1289.0 9.1 add_add_fusion.3
  1299.4 5.7 fusion.97
  1308.4 5.7 fusion.92
  1314.1 5.7 fusion.96
  1328.2 327.4 %all-reduce.10.cloned.1.call-done = f32[2048,1280]{1,0:T(8,128)} async-done(((f32[2048,1280]{1,0:T(8,128)}), f32[2048,1280]{1,0:T(8,128)}) %all-reduce.10.cloned.1.call-update) | async-done | bytes 10485776 | tf_op jit(solution)/shard_map/psum | solution.py:174
  1655.7 7.9 fusion.82
  1663.7 9.8 fusion.65
  1673.6 12.9 convert_reduce_fusion.1
  1686.5 26.9 %all-reduce = (f32[1280]{0:T(1024)}, f32[1280]{0:T(1024)}, f32[320]{0:T(512)}, f32[320]{0:T(512)}, f32[1280]{0:T(1024)}, /*index=5*/f32[1280]{0:T(1024)}, f32[1280]{0:T(1024)}, f32[320]{0:T(512)}, f32[1280]{0:T(1024)}) all-reduce(f32[1280]{0:T(1024)S(1)} %get-tuple-element.187, ...), channel_id=1, replica_groups=mesh['dp'=8,'tensor'=4] {'dp'}, use_global_device_ids=true, to_apply=%region_20.21 | all-reduce | flops 8640 | bytes 69120 | tf_op jit(solution)/shard_map/psum | solution.py:194
  1713.4 92.8 %all-reduce.12.cloned.1.call-done = (f32[1280,320]{0,1:T(8,128)}, f32[1280,320]{0,1:T(8,128)}, f32[1280,320]{0,1:T(8,128)}, f32[320,1280]{1,0:T(8,128)}, f32[1280,320]{0,1:T(8,128)}, /*index=5*/f32[320,1280]{1,0:T(8,128)}) async-done(((f32[1280,320]{0,1:T(8,128)}, f32[1280,320]{0,1:T(8,128)}, f32[1280,320]{0,1:T(8,128)}, f32[320,1280]{1,0:T(8,128)}, f32[1280,320]{0,1:T(8,128)}, ...) | async-done | bytes 9830416 | tf_op jit(solution)/shard_map/psum | solution.py:194
  (314 shorter events, 157.4 us)
Async XLA Ops:
  7.2 450.6 %copy-start = (bf16[320,1280]{1,0:T(8,128)(2,1)S(1)}, bf16[320,1280]{1,0:T(8,128)(2,1)}, u32[]{:S(2)}) copy-start(bf16[320,1280]{1,0:T(8,128)(2,1)} %param.37) | copy-start | bytes 2457604
  7.2 427.0 %all-reduce.8.cloned.1.call-start = ((), (), s32[]{:S(2)}) async-start(), calls=%async_computation | async-start | bytes 20971520 | tf_op jit(solution)/shard_map/psum | solution.py:123
  72.8 361.3 %copy-start.69 = (f32[1280]{0:T(1024)S(1)}, f32[1280]{0:T(1024)}, u32[]{:S(2)}) copy-start(f32[1280]{0:T(1024)} %param.32) | copy-start | bytes 15364
  72.8 1106.0 %all-reduce.14.cloned.1.call-start = ((), (), s32[]{:S(2)}) async-start(), calls=%async_computation.3 | async-start | bytes 41943040 | tf_op jit(solution)/shard_map/psum | solution.py:131
  480.9 697.9 %copy-start.71 = (f32[1280]{0:T(1024)S(1)}, f32[1280]{0:T(1024)}, u32[]{:S(2)}) copy-start(f32[1280]{0:T(1024)} %param.38) | copy-start | bytes 15364
  481.0 1174.7 %all-reduce.10.cloned.1.call-start = ((), (), s32[]{:S(2)}) async-start(), calls=%async_computation.1 | async-start | bytes 20971520 | tf_op jit(solution)/shard_map/psum | solution.py:174
  1178.8 15.8 slice-start
  1178.8 15.8 slice-start.8
  1178.8 15.8 slice-start.1
  1178.8 16.2 slice-start.2
  1178.8 17.4 slice-start.9
  1178.8 18.0 slice-start.10
  1298.1 508.1 %all-reduce.12.cloned.1.call-start = ((), (), s32[]{:S(2)}) async-start(), calls=%async_computation.2 | async-start | bytes 19660800 | tf_op jit(solution)/shard_map/psum | solution.py:194
  1308.4 11.4 slice-start.15
  1325.9 329.7 %copy-start.51 = (f32[2048]{0:T(1024)S(1)}, f32[2048]{0:T(1024)}, u32[]{:S(2)}) copy-start(f32[2048]{0:T(1024)} %copy-done.50) | copy-start | bytes 24580
  1325.9 329.7 %copy-start.54 = (f32[1280]{0:T(1024)S(1)}, f32[1280]{0:T(1024)}, u32[]{:S(2)}) copy-start(f32[1280]{0:T(1024)} %param.24) | copy-start | bytes 15364
  1328.2 335.4 %copy-start.61 = (f32[2048]{0:T(1024)S(1)}, f32[2048]{0:T(1024)}, u32[]{:S(2)}) copy-start(f32[2048]{0:T(1024)} %copy-done.60) | copy-start | bytes 24580
  1328.2 335.4 %copy-start.56 = (f32[2048]{0:T(1024)S(1)}, f32[2048]{0:T(1024)}, u32[]{:S(2)}) copy-start(f32[2048]{0:T(1024)} %copy-done.55) | copy-start | bytes 24580
  1655.6 17.9 slice-start.5
  1655.7 17.9 slice-start.6
  1673.6 12.9 copy-start.62
  1673.6 12.9 copy-start.63
  1673.6 12.9 copy-start.64
  1673.6 12.9 copy-start.73
  (85 other events, 324.7 us)
Sparse Core Ops, SparseCore 0:
  73.0 361.1 all-reduce.7
  481.1 697.6 all-reduce.13
  1298.2 357.3 all-reduce.9
  1662.0 144.1 all-reduce.11
where the time goes:
time: 1830 us; the launch traced here: 1820 us
  waiting for transfers between devices  1480 us (81%)
  matrix products  130 us (7%)
  other arithmetic  109 us (6%)
  local copies, waits for them, and re-layouts  60.1 us (3%)
  blocking collectives  26.9 us (1%)
    psum x1, waiting for transfers between devices, shards(): lax.psum(jnp.dot(act, proj_weight, preferred_element_type=jnp.float32), '...  698 us
    psum x1, waiting for transfers between devices, shards(): lax.psum(jnp.dot(mixed, out_weight, preferred_element_type=jnp.float32),...  361 us
    psum x1, waiting for transfers between devices, shards(): d_normed1 = lax.psum(partial_in, 'tensor')  327 us
    psum x1, waiting for transfers between devices, shards(): lax.psum((grad_g1, grad_c1, grad_wq, grad_bq, grad_wk, grad_wv, grad_bv,...  92.8 us
  transfers between devices with their start and end apart: 4, of which 4 were waited for; matrix products, arithmetic and copies ran while one was open for 3% of the time, Pallas kernels for 0%

commit v1 on v0

v1 whole, which is shorter than its diff:
```python
import functools
import math

import jax
import jax.numpy as jnp
from jax import lax
from jax.experimental import pallas as pl
from jax.experimental.pallas import tpu as pltpu
from jax.sharding import PartitionSpec as P

HEAD_DIM = 160
MAX_DOC = 512
EPS = 1e-05
NEG = -1e30
BLK = 256
WIN = 256
LANES = 128
SCALE = 1.0 / math.sqrt(HEAD_DIM)
LOG2E = 1.0 / math.log(2.0)
BF = jnp.bfloat16
F32 = jnp.float32
VMEM_MAX = 60 << 20


def nn(a, b):
    return lax.dot_general(a, b, (((1,), (0,)), ((), ())), preferred_element_type=F32)


def nt(a, b):
    return lax.dot_general(a, b, (((1,), (1,)), ((), ())), preferred_element_type=F32)


def tn(a, b):
    return lax.dot_general(a, b, (((0,), (0,)), ((), ())), preferred_element_type=F32)


def whole(shape):
    return pl.BlockSpec(shape, lambda *_: (0,) * len(shape), pipeline_mode=pl.Buffered(1))


def held(shape):
    return pl.BlockSpec(shape, lambda *_: (0,) * len(shape))


def rows(width):
    return pl.BlockSpec((BLK, width), lambda i: (i, 0))


def column_of(row):
    n = row.shape[1]
    eye = lax.broadcasted_iota(jnp.int32, (n, n), 0) == lax.broadcasted_iota(jnp.int32, (n, n), 1)
    return jnp.sum(jnp.where(eye, row, jnp.zeros_like(row)), axis=1, keepdims=True)


def fold8(t):
    return jnp.sum(t.reshape(t.shape[0] // 8, 8, t.shape[1]), axis=0)


def params(grid, vmem=VMEM_MAX):
    return pltpu.CompilerParams(dimension_semantics=("arbitrary",) * grid, vmem_limit_bytes=vmem)


def normalize(v):
    center = v - jnp.mean(v, axis=-1, keepdims=True)
    inv = lax.rsqrt(jnp.mean(center * center, axis=-1, keepdims=True) + EPS)
    return center * inv, inv


def project_kernel(x_ref, g_ref, c_ref, wq_ref, wk_ref, wv_ref, bq_ref, bv_ref, n_ref, q_ref, k_ref, v_ref):
    hat, _ = normalize(x_ref[...].astype(F32))
    normed = (hat * g_ref[...] + c_ref[...]).astype(BF)
    n_ref[...] = normed
    q_ref[...] = (nt(normed, wq_ref[...]) + bq_ref[...]).astype(BF)
    k_ref[...] = nt(normed, wk_ref[...]).astype(BF)
    v_ref[...] = (nt(normed, wv_ref[...]) + bv_ref[...]).astype(BF)


def project(x, g1, c1, wq, wk, wv, bq, bv):
    tokens, width = x.shape
    out = wq.shape[0]
    return pl.pallas_call(
        project_kernel,
        grid=(tokens // BLK,),
        in_specs=[rows(width), whole((1, width)), whole((1, width))]
        + [whole((out, width))] * 3
        + [whole((1, out))] * 2,
        out_specs=[rows(width)] + [rows(out)] * 3,
        out_shape=[jax.ShapeDtypeStruct((tokens, width), BF)] + [jax.ShapeDtypeStruct((tokens, out), BF)] * 3,
        compiler_params=params(1),
        cost_estimate=pl.CostEstimate(
            flops=6 * tokens * width * out, bytes_accessed=2 * (tokens * (2 * width + 3 * out) + 3 * width * out), transcendentals=0
        ),
        name="project",
    )(x, g1, c1, wq, wk, wv, bq, bv)


HEADS_IN_GROUP = 4
GROUP = HEADS_IN_GROUP * HEAD_DIM


def window_of(head):
    low = head * HEAD_DIM
    start = low // LANES * LANES
    return start, low - start


def lane_mask(offset):
    lane = lax.broadcasted_iota(jnp.int32, (1, WIN), 1)
    return (lane >= offset) & (lane < offset + HEAD_DIM)


def spread(parts):
    tiles = [None] * (GROUP // LANES)
    for head, part in enumerate(parts):
        first = window_of(head)[0] // LANES
        for half in range(WIN // LANES):
            piece = part[:, half * LANES : (half + 1) * LANES]
            at = first + half
            tiles[at] = piece if tiles[at] is None else tiles[at] + piece
    return jnp.concatenate(tiles, axis=1)


def attend_kernel(seg_s, q_ref, k_ref, v_ref, seg_ref, o_ref, lse_ref, bias):
    s, i = pl.program_id(0), pl.program_id(1)
    groups = q_ref.shape[1] // GROUP
    back = MAX_DOC // BLK
    lead = seg_s[s, i * BLK]
    count = jnp.int32(1)
    for d in range(1, back + 1):
        last = seg_s[s, jnp.maximum((i - d + 1) * BLK - 1, 0)]
        count = count + jnp.where((i >= d) & (last == lead), 1, 0)
    seg_col = column_of(seg_ref[0, :, pl.ds(pl.multiple_of(i * BLK, BLK), BLK)])

    def body(blocks):
        keys = blocks * BLK
        start = pl.multiple_of((i + 1 - blocks) * BLK, BLK)
        row = i * BLK + lax.broadcasted_iota(jnp.int32, (BLK, keys), 0)
        col = start + lax.broadcasted_iota(jnp.int32, (BLK, keys), 1)
        allowed = (row >= col) & (seg_col == seg_ref[0, :, pl.ds(start, keys)])
        bias[:, :keys] = jnp.where(allowed, 0.0, NEG)

        def group(gi, _):
            parts = []
            lse = lse_ref[...]
            head_lane = lax.broadcasted_iota(jnp.int32, (1, LANES), 1)
            for h in range(HEADS_IN_GROUP):
                at, off = window_of(h)
                lanes = pl.ds(pl.multiple_of(gi * GROUP + at, LANES), WIN)
                mask = lane_mask(off)
                q = q_ref[:, lanes]
                q = jnp.where(mask, q, jnp.zeros_like(q))
                t = nt(q, k_ref[pl.ds(start, keys), lanes]) * (SCALE * LOG2E) + bias[:, :keys]
                top = jnp.max(t, axis=1, keepdims=True)
                p = jnp.exp2(t - top)
                total = jnp.sum(p, axis=1, keepdims=True)
                o = nn(p.astype(BF), v_ref[pl.ds(start, keys), lanes])
                parts.append(jnp.where(mask, o * (1.0 / total), 0.0))
                lse = jnp.where(head_lane == gi * HEADS_IN_GROUP + h, top + jnp.log2(total), lse)
            lse_ref[...] = lse
            o_ref[:, pl.ds(pl.multiple_of(gi * GROUP, LANES), GROUP)] = spread(parts).astype(BF)
            return 0

        lax.fori_loop(0, groups, group, 0)

    lse_ref[...] = jnp.zeros_like(lse_ref)
    for blocks in range(1, back + 2):
        pl.when(count == blocks)(functools.partial(body, blocks))


def attend(q, k, v, seg):
    tokens, width = q.shape
    seqs, length = seg.shape
    n = length // BLK
    spec_q = pl.BlockSpec((BLK, width), lambda s, i, _: (s * n + i, 0))
    spec_k = pl.BlockSpec((length, width), lambda s, i, _: (s, 0))
    pairs = seqs * n * 2.5 * BLK * BLK * (width // HEAD_DIM)
    return pl.pallas_call(
        attend_kernel,
        grid_spec=pltpu.PrefetchScalarGridSpec(
            num_scalar_prefetch=1,
            grid=(seqs, n),
            in_specs=[spec_q, spec_k, spec_k, pl.BlockSpec((1, 1, length), lambda s, i, _: (s, 0, 0))],
            out_specs=[spec_q, pl.BlockSpec((BLK, LANES), lambda s, i, _: (s * n + i, 0))],
            scratch_shapes=[pltpu.VMEM((BLK, BLK + MAX_DOC), F32)],
        ),
        out_shape=[jax.ShapeDtypeStruct((tokens, width), BF), jax.ShapeDtypeStruct((tokens, LANES), F32)],
        compiler_params=params(2),
        cost_estimate=pl.CostEstimate(
            flops=int(pairs * 8 * WIN), bytes_accessed=8 * tokens * width, transcendentals=int(pairs)
        ),
        name="attend",
    )(seg, q, k, v, seg.reshape(seqs, 1, length))


def attend_back_kernel(
    seg_s, q_ref, do_ref, o_ref, lse_ref, k_ref, v_ref, seg_ref, dq_ref, dk_ref, dv_ref, bias, dq_acc, lse_t, delta_t
):
    s, j = pl.program_id(0), pl.program_id(1)
    n = pl.num_programs(1)
    length, width = q_ref.shape
    groups = width // GROUP
    ahead = MAX_DOC // BLK

    @pl.when(j == 0)
    def _():
        dq_acc[...] = jnp.zeros_like(dq_acc)
        head = lax.broadcasted_iota(jnp.int32, (16, width), 0)
        lane = lax.broadcasted_iota(jnp.int32, (16, width), 1)
        pick = jnp.where((lane >= head * HEAD_DIM) & (lane < (head + 1) * HEAD_DIM), 1.0, 0.0).astype(BF)
        for b in range(length // BLK):
            at = slice(b * BLK, (b + 1) * BLK)
            lse_t[:, at] = lse_ref[at, :].T[:16, :]
            prod = do_ref[at, :].astype(F32) * o_ref[at, :].astype(F32)
            high = prod.astype(BF)
            rest = (prod - high.astype(F32)).astype(BF)
            delta_t[:, at] = nt(pick, high) + nt(pick, rest)

    tail = seg_s[s, (j + 1) * BLK - 1]
    count = jnp.int32(1)
    for d in range(1, ahead + 1):
        first = seg_s[s, jnp.minimum((j + d) * BLK, length - 1)]
        count = count + jnp.where((j + d < n) & (first == tail), 1, 0)
    start = pl.multiple_of(j * BLK, BLK)
    seg_col = column_of(seg_ref[0, :, pl.ds(start, BLK)])

    def body(blocks):
        queries = blocks * BLK
        span = pl.ds(start, queries)
        row = lax.broadcasted_iota(jnp.int32, (BLK, queries), 0)
        col = lax.broadcasted_iota(jnp.int32, (BLK, queries), 1)
        allowed = (row <= col) & (seg_col == seg_ref[0, :, span])
        bias[:, :queries] = jnp.where(allowed, 0.0, NEG)

        def group(gi, _):
            dks, dvs = [], []
            for h in range(HEADS_IN_GROUP):
                at, off = window_of(h)
                lanes = pl.ds(pl.multiple_of(gi * GROUP + at, LANES), WIN)
                mask = lane_mask(off)
                head = pl.ds(gi * HEADS_IN_GROUP + h, 1)
                k = k_ref[:, lanes]
                k = jnp.where(mask, k, jnp.zeros_like(k))
                v = v_ref[:, lanes]
                v = jnp.where(mask, v, jnp.zeros_like(v))
                q = q_ref[span, lanes]
                do = do_ref[span, lanes]
                t = nt(k, q) * (SCALE * LOG2E) + bias[:, :queries]
                p = jnp.exp2(t - lse_t[head, span])
                dvs.append(jnp.where(mask, nn(p.astype(BF), do), 0.0))
                ds = (p * (nt(v, do) - delta_t[head, span])).astype(BF)
                dks.append(jnp.where(mask, nn(ds, q), 0.0))
                dq_acc[span, lanes] += tn(ds, k)
            out = pl.ds(pl.multiple_of(gi * GROUP, LANES), GROUP)
            dk_ref[:, out] = (spread(dks) * SCALE).astype(BF)
            dv_ref[:, out] = spread(dvs).astype(BF)
            return 0

        lax.fori_loop(0, groups, group, 0)

    for blocks in range(1, ahead + 2):
        pl.when(count == blocks)(functools.partial(body, blocks))

    @pl.when(j == n - 1)
    def _():
        dq_ref[...] = (dq_acc[...] * SCALE).astype(BF)


def attend_back(q, k, v, seg, mixed, d_mixed, lse):
    tokens, width = q.shape
    seqs, length = seg.shape
    n = length // BLK
    spec_k = pl.BlockSpec((BLK, width), lambda s, j, _: (s * n + j, 0))
    spec_q = pl.BlockSpec((length, width), lambda s, j, _: (s, 0))
    pairs = seqs * n * 2.5 * BLK * BLK * (width // HEAD_DIM)
    return pl.pallas_call(
        attend_back_kernel,
        grid_spec=pltpu.PrefetchScalarGridSpec(
            num_scalar_prefetch=1,
            grid=(seqs, n),
            in_specs=[
                spec_q,
                spec_q,
                spec_q,
                pl.BlockSpec((length, LANES), lambda s, j, _: (s, 0)),
                spec_k,
                spec_k,
                pl.BlockSpec((1, 1, length), lambda s, j, _: (s, 0, 0)),
            ],
            out_specs=[spec_q, spec_k, spec_k],
            scratch_shapes=[
                pltpu.VMEM((BLK, BLK + MAX_DOC), F32),
                pltpu.VMEM((length, width), F32),
                pltpu.VMEM((16, length), F32),
                pltpu.VMEM((16, length), F32),
            ],
        ),
        out_shape=[jax.ShapeDtypeStruct((tokens, width), BF)] * 3,
        compiler_params=params(2),
        cost_estimate=pl.CostEstimate(
            flops=int(pairs * 20 * WIN), bytes_accessed=16 * tokens * width, transcendentals=int(pairs)
        ),
        name="attend_back",
    )(seg, q, d_mixed, mixed, lse, k, v, seg.reshape(seqs, 1, length))


def middle_kernel(
    own, m_ref, x_ref, g_ref, w_ref, wo_ref, w1_ref, w2_ref, bo_ref, g2_ref, c2_ref, b1_ref, b2_ref,
    y_ref, dr_ref, dm_ref, gwo_ref, gw1_ref, gw2_ref, vec_ref, sq_ref,
):
    i = pl.program_id(0)

    @pl.when(i == 0)
    def _():
        for ref in (gwo_ref, gw1_ref, gw2_ref, vec_ref):
            ref[...] = jnp.zeros_like(ref)

    mixed = m_ref[...]
    cot = g_ref[...]
    attended = nn(mixed, wo_ref[...]) + bo_ref[...]
    resid = x_ref[...].astype(F32) + attended
    hat, inv = normalize(resid)
    normed = (hat * g2_ref[...] + c2_ref[...]).astype(BF)
    pre = nt(normed, w1_ref[...]) + b1_ref[...]
    cdf = 0.5 + 0.5 * lax.erf(pre * math.sqrt(0.5))
    act = (pre * cdf).astype(BF)
    slope = cdf + pre * jnp.exp(-0.5 * pre * pre) * (1.0 / math.sqrt(2.0 * math.pi))
    branch = nn(act, w2_ref[...]) + b2_ref[...]
    output = resid + branch
    y_ref[...] = output.astype(BF)
    weight = column_of(w_ref[0])
    lane = lax.broadcasted_iota(jnp.int32, (1, LANES), 1)
    sums = jnp.zeros((1, LANES), F32)
    for at, v in enumerate((attended, branch, output)):
        one = jnp.sum(weight * jnp.sum(v * v, axis=1, keepdims=True), axis=0, keepdims=True)
        sums = jnp.where(lane == at, one, sums)
    sq_ref[...] = jnp.broadcast_to(sums, sq_ref.shape[1:])[None]

    d_pre = (nt(cot, w2_ref[...]) * slope).astype(BF)
    gw2_ref[...] += tn(act[:, :own], cot)
    gw1_ref[...] += tn(d_pre[:, :own], normed)
    d_normed = nn(d_pre, w1_ref[...])
    d_hat = d_normed * g2_ref[...]
    grad = cot.astype(F32)
    d_resid = grad + inv * (
        d_hat - jnp.mean(d_hat, axis=1, keepdims=True) - hat * jnp.mean(d_hat * hat, axis=1, keepdims=True)
    )
    dr_ref[...] = d_resid
    low = d_resid.astype(BF)
    gwo_ref[...] += tn(mixed[:, :own], low)
    dm_ref[...] = nt(low, wo_ref[...]).astype(BF)
    for at, v in enumerate((grad, d_pre.astype(F32), d_normed * hat, d_normed, low.astype(F32))):
        vec_ref[at] += fold8(v)


def middle(own, mixed, x, cot, valid, wo, w1, w2, bo, g2, c2, b1, b2):
    tokens, width = x.shape
    inner, hidden = wo.shape[0], w1.shape[0]
    n = tokens // BLK
    return pl.pallas_call(
        functools.partial(middle_kernel, own),
        grid=(n,),
        in_specs=[rows(inner), rows(width), rows(width), pl.BlockSpec((1, 1, BLK), lambda i: (i, 0, 0))]
        + [whole((inner, width)), whole((hidden, width)), whole((hidden, width))]
        + [whole((1, width))] * 3
        + [whole((1, hidden)), whole((1, width))],
        out_specs=[rows(width), rows(width), rows(inner)]
        + [held((own, width))] * 3
        + [held((5, 8, width)), pl.BlockSpec((1, 8, LANES), lambda i: (i, 0, 0))],
        out_shape=[
            jax.ShapeDtypeStruct((tokens, width), BF),
            jax.ShapeDtypeStruct((tokens, width), F32),
            jax.ShapeDtypeStruct((tokens, inner), BF),
        ]
        + [jax.ShapeDtypeStruct((own, width), F32)] * 3
        + [jax.ShapeDtypeStruct((5, 8, width), F32), jax.ShapeDtypeStruct((n, 8, LANES), F32)],
        compiler_params=params(1),
        cost_estimate=pl.CostEstimate(
            flops=2 * tokens * width * (6 * width + 3 * own),
            bytes_accessed=14 * tokens * width + 6 * width * width,
            transcendentals=2 * tokens * hidden,
        ),
        name="middle",
    )(mixed, x, cot, valid.astype(F32).reshape(n, 1, BLK), wo, w1, w2, bo, g2, c2, b1, b2)


def finish_kernel(dq_ref, dk_ref, dv_ref, x_ref, dr_ref, g_ref, wq_ref, wk_ref, wv_ref, dx_ref, vec_ref):
    @pl.when(pl.program_id(0) == 0)
    def _():
        vec_ref[...] = jnp.zeros_like(vec_ref)

    d_normed = nn(dq_ref[...], wq_ref[...]) + nn(dk_ref[...], wk_ref[...]) + nn(dv_ref[...], wv_ref[...])
    hat, inv = normalize(x_ref[...].astype(F32))
    d_hat = d_normed * g_ref[...]
    dx_ref[...] = dr_ref[...] + inv * (
        d_hat - jnp.mean(d_hat, axis=1, keepdims=True) - hat * jnp.mean(d_hat * hat, axis=1, keepdims=True)
    )
    vec_ref[0] += fold8(d_normed * hat)
    vec_ref[1] += fold8(d_normed)


def finish(dq, dk, dv, x, d_resid, g1, wq, wk, wv):
    tokens, width = x.shape
    inner = wq.shape[0]
    return pl.pallas_call(
        finish_kernel,
        grid=(tokens // BLK,),
        in_specs=[rows(inner)] * 3 + [rows(width), rows(width), whole((1, width))] + [whole((inner, width))] * 3,
        out_specs=[rows(width), held((2, 8, width))],
        out_shape=[jax.ShapeDtypeStruct((tokens, width), F32), jax.ShapeDtypeStruct((2, 8, width), F32)],
        compiler_params=params(1),
        cost_estimate=pl.CostEstimate(
            flops=6 * tokens * width * inner, bytes_accessed=16 * tokens * width + 6 * width * inner, transcendentals=0
        ),
        name="finish",
    )(dq, dk, dv, x, d_resid, g1, wq, wk, wv)


def round_kernel(x_ref, o_ref):
    o_ref[...] = x_ref[...].astype(BF)


def round_rows(t):
    count, width = t.shape
    return pl.pallas_call(
        round_kernel,
        grid=(pl.cdiv(count, BLK),),
        in_specs=[rows(width)],
        out_specs=rows(width),
        out_shape=jax.ShapeDtypeStruct(t.shape, BF),
        compiler_params=params(1),
        name="round_rows",
    )(t)


def gather(parts, extra, dp, tp):
    own, width = parts[0].shape
    piece = own // dp
    mine = jnp.stack([t.reshape(dp, piece, width) for t in parts], axis=1)
    mine = lax.dynamic_index_in_dim(mine, lax.axis_index("dp"), 0, keepdims=False).astype(F32)
    mine = mine.reshape(len(parts) * piece, width)
    if extra is not None:
        mine = jnp.concatenate([mine, extra], axis=0)
    full = lax.all_gather(mine, ("tensor", "dp"))
    full = full.reshape(tp, dp, -1, width)
    vecs = full[:, 0, len(parts) * piece :]
    full = round_rows(full.reshape(-1, width)).reshape(full.shape)
    twice = jnp.concatenate([full, full], axis=0)
    full = lax.dynamic_slice_in_dim(twice, lax.axis_index("tensor"), tp, 0)
    count = len(parts) * piece
    body = full[:, :, :count].reshape(tp, dp, len(parts), piece, width)
    wholes = [body[:, :, m].reshape(tp * own, width) for m in range(len(parts))]
    vecs = jnp.concatenate([vecs, vecs], axis=0)
    return wholes, lax.dynamic_slice_in_dim(vecs, lax.axis_index("tensor"), tp, 0)


def shards(dp, tp, x, g1, c1, wq, bq, wk, wv, bv, wo, bo, g2, c2, w1, b1, w2, b2, seg, valid, cot):
    tokens, width = x.shape
    seqs, length = seg.shape
    own = wq.shape[1]

    def line(t):
        return t.reshape(1, -1)

    biases = jnp.concatenate([bq, bv, b1]).reshape(3, own)
    extra = jnp.zeros((8, width), F32).at[:3, :own].set(biases)
    (fq, fk, fv), more = gather([wq.T, wk.T, wv.T], extra, dp, tp)
    (fo, f1, f2), _ = gather([wo, w1.T, w2], None, dp, tp)
    abq, abv, ab1 = (line(more[:, r, :own]) for r in range(3))

    normed1, q, k, v = project(x, line(g1), line(c1), fq, fk, fv, abq, abv)
    mixed, lse = attend(q, k, v, seg)
    y, d_resid, d_mixed, gwo, gw1, gw2, vec, sq = middle(
        own, mixed, x, cot, valid, fo, f1, f2, line(bo), line(g2), line(c2), ab1, line(b2)
    )
    dq, dk, dv = attend_back(q, k, v, seg, mixed, d_mixed, lse)
    mine = [t[:, :own] for t in (dq, dk, dv)]
    gq, gk, gv = (tn(t, normed1) for t in mine)
    gbq, gbv = (jnp.sum(t.astype(F32), axis=0) for t in (mine[0], mine[2]))
    grad_input, last = finish(dq, dk, dv, x, d_resid, line(g1), fq, fk, fv)

    weight = valid.astype(F32)
    counted = jnp.maximum(jnp.sum(weight, axis=1), 1.0) * width
    stat = jnp.sum(sq[:, 0, :3].reshape(seqs, length // BLK, 3), axis=1)
    rms = jnp.sqrt(stat / counted[:, None])

    vec = jnp.sum(vec, axis=1)
    last = jnp.sum(last, axis=1)
    big = lax.psum((gwo, gw1, gw2), "dp")
    mats = lax.psum((gq, gk, gv), "dp")
    gb2, gb1, gg2, gc2, gbo, gg1, gc1, gbq, gbv = lax.psum(
        (vec[0], vec[1, :own], vec[2], vec[3], vec[4], last[0], last[1], gbq, gbv), "dp"
    )
    gwo, gw1, gw2 = big
    gq, gk, gv = mats
    return (
        y, grad_input, gg1, gc1, gq.T, gbq, gk.T, gv.T, gbv, gwo, gbo, gg2, gc2, gw1.T, gb1, gw2, gb2, rms,
    )


def solution(mesh):
    dp, tp = mesh.shape["dp"], mesh.shape["tensor"]
    tok, col, row, vec, rep = P("dp", None), P(None, "tensor"), P("tensor", None), P("tensor"), P()
    return jax.shard_map(
        functools.partial(shards, dp, tp),
        mesh=mesh,
        in_specs=(tok, rep, rep, col, vec, col, col, vec, row, rep, rep, rep, col, vec, row, rep, tok, tok, tok),
        out_specs=(tok, tok, rep, rep, col, vec, col, col, vec, row, rep, rep, rep, col, vec, row, rep, tok),
        check_vma=False,
    )
```

time: 1830 us -> 672 us (0.37)
  waiting for transfers between devices: 1480 us -> 324 us
  Pallas kernels: 0 us -> 230 us
  matrix products: 130 us -> 16.8 us
  other arithmetic: 109 us -> 24.3 us
  local copies, waits for them, and re-layouts: 60.1 us -> 31.6 us
    psum x4 -> x1, waiting for transfers between devices: 1480 us -> 77.9 us  [shards(): mats = lax.psum((gq, gk, gv), 'dp')]
    all_gather x0 -> x2, waiting for transfers between devices: none -> 246 us  [gather(): full = lax.all_gather(mine, ('tensor', 'dp'))]
    pallas_call x0 -> x7, Pallas kernels: none -> 230 us  [the longest x1 67.6 us: middle(): pl.pallas_call(functools.partial(middle_kernel, own), grid=(n,), in_specs...]
    dot_general x32 -> x3, matrix products: 130 us -> 16.8 us  [tn(): lax.dot_general(a, b, (((0,), (0,)), ((), ())), preferred_element_type=F32)]
    reduce_sum x13 -> x5, other arithmetic: 84.9 us -> 4.49 us  [the longest x2 3.49 us: shards(): gbq, gbv = (jnp.sum(t.astype(F32), axis=0) for t in (mine[0], mine[2]))]
    convert_element_type x5 -> x3, other arithmetic: 21.5 us -> 0.95 us  [the longest x2 0.95 us: gather(): lax.dynamic_index_in_dim(mine, lax.axis_index('dp'), 0, keepdims=False)]
    while x52 -> x0, local copies, waits for them, and re-layouts: 19.1 us -> none  [the longest x4 7.14 us: shards(): lax.map(lambda t: attend_backward(t[0], t[1], t[2], t[3], t[4], t[5]), (s...]
  transfers between devices with their start and end apart: 4 -> 3, of which waited for: 4 -> 3; matrix products, arithmetic and copies ran while one was open for 3% -> 2% of each run, Pallas kernels for 0% -> 7%
where the time goes in v1:
time: 672 us; the launch traced here: 671 us
  waiting for transfers between devices  324 us (48%)
  Pallas kernels  230 us (34%)
  local copies, waits for them, and re-layouts  31.6 us (5%)
  blocking collectives  29.9 us (4%)
  other arithmetic  24.3 us (4%)
  matrix products  16.8 us (2%)
  between operations  14 us (2%)
    all_gather x2, waiting for transfers between devices, gather(): full = lax.all_gather(mine, ('tensor', 'dp'))  246 us
    psum x1, waiting for transfers between devices, shards(): mats = lax.psum((gq, gk, gv), 'dp')  77.9 us
    pallas_call x1, Pallas kernels, middle(): pl.pallas_call(functools.partial(middle_kernel, own), grid=(n,), in_specs...  67.6 us
    pallas_call x1, Pallas kernels, attend_back(): pl.pallas_call(attend_back_kernel, grid_spec=pltpu.PrefetchScalarGridSpec...  44.1 us
    pallas_call x2, Pallas kernels, round_rows(): pl.pallas_call(round_kernel, grid=(pl.cdiv(count, BLK),), in_specs=[rows(...  32.1 us
    pallas_call x1, Pallas kernels, finish(): pl.pallas_call(finish_kernel, grid=(tokens // BLK,), in_specs=[rows(inner...  32.1 us
    psum x1, blocking collectives, shards(): lax.psum((vec[0], vec[1, :own], vec[2], vec[3], vec[4], last[0], last[1],...  29.9 us
    pallas_call x1, Pallas kernels, project(): pl.pallas_call(project_kernel, grid=(tokens // BLK,), in_specs=[rows(widt...  29.6 us
  transfers between devices with their start and end apart: 3, of which 3 were waited for; matrix products, arithmetic and copies ran while one was open for 2% of the time, Pallas kernels for 7%

profile of v1, /device:TPU:0, one launch (start us, length us, event | category | flops | bytes accessed | tf_op | source)
XLA Modules:
  0.0 670.7 jit_solution(14748966220325344242)
XLA Ops:
  17.1 125.5 %all-gather.4.cloned.1.call-done = f32[32,120,1280]{2,1,0:T(8,128)} async-done(((f32[1,120,1280]{2,1,0:T(8,128)}), f32[32,120,1280]{2,1,0:T(8,128)}) %all-gather.4.cloned.1.call-update) | async-done | bytes 19660816 | tf_op jit(solution)/shard_map/all_gather | solution.py:443
  142.6 15.9 %round_rows.3 = bf16[3840,1280]{1,0:T(8,128)(2,1)} custom-call(f32[3840,1280]{1,0:T(8,128)} %bitcast.63), custom_call_target="tpu_custom_call" | custom-call | tf_op jit(solution)/shard_map/round_rows/pallas_call | solution.py:424
  158.5 120.2 %all-gather.6.cloned.1.call-done.x_ref = f32[4096,1280]{1,0:T(8,128)} async-done(((f32[128,1280]{1,0:T(8,128)}), f32[4096,1280]{1,0:T(8,128)}) %all-gather.6.cloned.1.call-update) | async-done | bytes 20971536 | tf_op jit(solution)/shard_map/all_gather | solution.py:443
  278.7 16.2 %round_rows.2 = bf16[4096,1280]{1,0:T(8,128)(2,1)} custom-call(f32[4096,1280]{1,0:T(8,128)} %all-gather.6.cloned.1.call-done.x_ref), custom_call_target="tpu_custom_call" | custom-call | tf_op jit(solution)/shard_map/round_rows/pallas_call | solution.py:424
  294.9 14.8 %fusion = (bf16[4,8,120,1280]{3,2,1,0:T(8,128)(2,1)}, bf16[4,8,120,1280]{3,2,1,0:T(8,128)(2,1)S(1)}) fusion(s32[]{:T(128)S(6)} %select_n.11, bf16[4,8,120,1280]{3,2,1,0:T(8,128)(2,1)} %bitcast.59, bf16[4,8,128,1280]{3,2,1,0:T(8,128)(2,1)} %bitcast.58), kind=kLoop, calls=%fused_computation.4 | loop fusion | flops 9830400 | bytes 39976964 | tf_op jit(solution)/shard_map/concatenate | solution.py:447
  309.7 3.9 fusion.14
  316.1 7.1 %fusion.13 = (bf16[4,8,1,40,1280]{4,3,2,1,0:T(8,128)(2,1)}, bf16[4,8,1,40,1280]{4,3,2,1,0:T(8,128)(2,1)}, bf16[4,8,1,40,1280]{4,3,2,1,0:T(8,128)(2,1)}) fusion(bf16[4,8,3,40,1280]{4,3,2,1,0:T(8,128)(2,1)} %bitcast.60), kind=kLoop, calls=%fused_computation.43 | loop fusion | bytes 19660800 | tf_op jit(solution)/shard_map/slice | solution.py:451
  323.9 29.6 %project.1 = (bf16[2048,1280]{1,0:T(8,128)(2,1)}, bf16[2048,1280]{1,0:T(8,128)(2,1)}, bf16[2048,1280]{1,0:T(8,128)(2,1)}, bf16[2048,1280]{1,0:T(8,128)(2,1)}) custom-call(bf16[2048,1280]{1,0:T(8,128)(2,1)} %x_ref.5, f32[1,1280]{1,0:T(1,128)} %reshape.131.g_ref, f32[1,1280]{1,0:T(1,128)} %reshape.132.c_ref, bf16[1280,1280]{1,0:T(8,128)(2,1)} %bitcast.68, ...), custom_call_target="tpu_custom_call" | custom-call | flops 20132659200 | bytes 36044800 | tf_op jit(solution)/shard_map/project/pallas_call | solution.py:81
  353.6 24.7 %attend.1 = (bf16[2048,1280]{1,0:T(8,128)(2,1)}, f32[2048,128]{1,0:T(8,128)}) custom-call(s32[2,1024]{1,0:T(2,128)} %seg_s.3, bf16[2048,1280]{1,0:T(8,128)(2,1)} %get-tuple-element.49.q_ref, bf16[2048,1280]{1,0:T(8,128)(2,1)} %get-tuple-element.50.k_ref, bf16[2048,1280]{1,0:T(8,128)(2,1)} %get-tuple-element.51.v_ref, s32[2,1,1024]{2,1,0:T(1,128)} %reshape.137.seg_ref), custom_call_target="tpu_custom_call" | custom-call | flops 21474836480 | bytes 20971520 | tf_op jit(solution)/shard_map/attend/pallas_call | solution.py:177
  378.3 67.6 %middle.1 = (bf16[2048,1280]{1,0:T(8,128)(2,1)}, f32[2048,1280]{1,0:T(8,128)}, bf16[2048,1280]{1,0:T(8,128)(2,1)}, f32[320,1280]{1,0:T(8,128)}, f32[320,1280]{1,...) custom-call(bf16[2048,1280]{1,0:T(8,128)(2,1)} %get-tuple-element.52.m_ref.o_ref, ...), custom_call_target="tpu_custom_call" | custom-call | flops 45298483200 | bytes 46530560 | tf_op jit(solution)/shard_map/middle/pallas_call | solution.py:359
  445.9 44.1 %attend_back.1 = (bf16[2048,1280]{1,0:T(8,128)(2,1)}, bf16[2048,1280]{1,0:T(8,128)(2,1)}, bf16[2048,1280]{1,0:T(8,128)(2,1)}) custom-call(s32[2,1024]{1,0:T(2,128)} %seg_s.3, bf16[2048,1280]{1,0:T(8,128)(2,1)} %get-tuple-element.49.q_ref, bf16[2048,1280]{1,0:T(8,128)(2,1)} %get-tuple-element.54.do_ref, bf16[2048,1280]{1,0:T(8,128)(2,1)} %get-tuple-element.52.m_ref.o_ref, ...), custom_call_target="tpu_custom_call" | custom-call | flops 53687091200 | bytes 41943040 | tf_op jit(solution)/shard_map/attend_back/pallas_call | solution.py:275
  490.0 6.2 fusion.4
  496.2 6.1 fusion.2
  502.3 4.6 fusion.6
  507.7 32.1 %finish.1 = (f32[2048,1280]{1,0:T(8,128)}, f32[2,8,1280]{2,1,0:T(8,128)}) custom-call(bf16[2048,1280]{1,0:T(8,128)(2,1)} %get-tuple-element.56.dq_ref, bf16[2048,1280]{1,0:T(8,128)(2,1)} %get-tuple-element.57.dk_ref, bf16[2048,1280]{1,0:T(8,128)(2,1)} %get-tuple-element.58.dv_ref, bf16[2048,1280]{1,0:T(8,128)(2,1)} %x_ref.5, ...), custom_call_target="tpu_custom_call" | custom-call | flops 20132659200 | bytes 51773440 | tf_op jit(solution)/shard_map/finish/pallas_call | solution.py:404
  542.4 1.7 convert_reduce_fusion
  544.2 1.7 convert_reduce_fusion.1
  545.9 29.9 %all-reduce.1 = (f32[1280]{0:T(1024)}, f32[1280]{0:T(1024)}, f32[320]{0:T(512)}, f32[320]{0:T(512)}, f32[1280]{0:T(1024)}, /*index=5*/f32[1280]{0:T(1024)}, f32[1280]{0:T(1024)}, f32[320]{0:T(512)}, f32[1280]{0:T(1024)}) all-reduce(f32[1280]{0:T(1024)S(1)} %get-tuple-element.91, ...), channel_id=1, replica_groups=mesh['dp'=8,'tensor'=4] {'dp'}, use_global_device_ids=true, to_apply=%region_1.2 | all-reduce | flops 8640 | bytes 69120 | tf_op jit(solution)/shard_map/psum | solution.py:490
  575.9 77.9 %all-reduce.5.cloned.1.call-done = (f32[1280,320]{0,1:T(8,128)}, f32[1280,320]{0,1:T(8,128)}, f32[1280,320]{0,1:T(8,128)}, f32[320,1280]{1,0:T(8,128)}, f32[1280,320]{0,1:T(8,128)}, /*index=5*/f32[320,1280]{1,0:T(8,128)}) async-done(((f32[1280,320]{0,1:T(8,128)}, f32[1280,320]{0,1:T(8,128)}, f32[1280,320]{0,1:T(8,128)}, f32[320,1280]{1,0:T(8,128)}, f32[1280,320]{0,1:T(8,128)}, ...) | async-done | bytes 9830416 | tf_op jit(solution)/shard_map/psum | solution.py:489
  653.8 2.8 copy.67
  656.7 2.8 copy.68
  659.5 1.2 copy.69
  660.6 1.2 copy.70
  663.0 1.2 copy.72
  (75 shorter events, 17.6 us)
Async XLA Ops:
  7.2 5.1 copy-start.8
  7.2 5.7 copy-start.9
  7.2 6.3 copy-start.7
  7.2 6.8 %copy-start.5 = (s32[2,1024]{1,0:T(2,128)S(1)}, s32[2,1024]{1,0:T(2,128)}, u32[]{:S(2)}) copy-start(s32[2,1024]{1,0:T(2,128)} %param.38) | copy-start | bytes 24580
  7.2 7.5 %copy-start.10 = (f32[1280]{0:T(1024)S(1)}, f32[1280]{0:T(1024)}, u32[]{:S(2)}) copy-start(f32[1280]{0:T(1024)} %param.30) | copy-start | bytes 15364
  7.2 8.1 %copy-start.11 = (f32[1280]{0:T(1024)S(1)}, f32[1280]{0:T(1024)}, u32[]{:S(2)}) copy-start(f32[1280]{0:T(1024)} %param.31) | copy-start | bytes 15364
  7.3 8.6 %copy-start.12 = (f32[1280]{0:T(1024)S(1)}, f32[1280]{0:T(1024)}, u32[]{:S(2)}) copy-start(f32[1280]{0:T(1024)} %param.32) | copy-start | bytes 15364
  7.3 9.2 %copy-start.13 = (f32[1280]{0:T(1024)S(1)}, f32[1280]{0:T(1024)}, u32[]{:S(2)}) copy-start(f32[1280]{0:T(1024)} %param.36) | copy-start | bytes 15364
  7.3 135.3 %all-gather.4.cloned.1.call-start = ((), (), s32[]{:S(2)}) async-start(), calls=%async_computation | async-start | bytes 20275200 | tf_op jit(solution)/shard_map/all_gather | solution.py:443
  9.3 269.4 %all-gather.6.cloned.1.call-start = ((), (), s32[]{:S(2)}) async-start(), calls=%async_computation.1 | async-start | bytes 21626880 | tf_op jit(solution)/shard_map/all_gather | solution.py:443
  12.2 641.6 %all-reduce.5.cloned.1.call-start = ((), (), s32[]{:S(2)}) async-start(), calls=%async_computation.2 | async-start | bytes 19660800 | tf_op jit(solution)/shard_map/psum | solution.py:489
  490.0 12.3 %slice-start = ((s8[5242880]{0:T(1024)(128)(4,1)}), s8[4194304]{0:T(1024)(128)(4,1)S(1)}, s32[]{:S(2)}) async-start(s8[5242880]{0:T(1024)(128)(4,1)} %bitcast.82), calls=%async_computation.3 | async-start | bytes 8388608
  496.2 6.1 slice-start.1
  506.8 0.7 copy-start.6
  507.7 33.0 %copy-start.4 = (f32[5,8,1280]{2,1,0:T(8,128)S(1)}, f32[5,8,1280]{2,1,0:T(8,128)}, u32[]{:S(2)}) copy-start(f32[5,8,1280]{2,1,0:T(8,128)} %get-tuple-element.64) | copy-start | bytes 614404
  653.8 5.7 copy-start.3
  653.8 6.8 %copy-start.2 = (f32[320,1280]{1,0:T(8,128)S(1)}, f32[320,1280]{1,0:T(8,128)}, u32[]{:S(2)}) copy-start(f32[320,1280]{1,0:T(8,128)} %get-tuple-element.127) | copy-start | bytes 4915204
  656.6 5.2 copy-start.1
  659.5 3.5 copy-start
Sparse Core Ops, SparseCore 0:
  11.6 130.9 all-gather.3
  146.0 132.6 all-gather.5
  507.0 146.7 all-reduce.4

commit v2 on v1

--- a/solution.py
+++ b/solution.py
@@ -415,42 +415,162 @@
     )(dq, dk, dv, x, d_resid, g1, wq, wk, wv)
 
 
-def round_kernel(x_ref, o_ref):
-    o_ref[...] = x_ref[...].astype(BF)
-
-
-def round_rows(t):
-    count, width = t.shape
+def sibling(index, bit):
+    return index + bit - 2 * bit * (index // bit % 2)
+
+
+def gather_kernel(
+    bits, chunks, count, mine_ref, local_ref, bias_ref, full_ref, biases_ref, land, sem_s, sem_r, bias_s, bias_r
+):
+    d, z = lax.axis_index("dp"), lax.axis_index("tensor")
+    first, second = bits
+    core = d % 2
+    spot = d // first % 2 + 2 * (d // second % 2)
+    piece = mine_ref.shape[1]
+    own = local_ref.shape[1]
+
+    def at(dp=None, tensor=None):
+        return {"dp": d if dp is None else dp, "tensor": z if tensor is None else tensor}
+
+    z_peer = [None, sibling(z, 1), sibling(z, 2), sibling(sibling(z, 1), 2)]
+    x_peer, y_peer, c_peer = sibling(d, first), sibling(d, second), sibling(d, 1)
+    x_spot, y_spot = sibling(spot, 1), sibling(spot, 2)
+    targets = [at(tensor=t) for t in z_peer[1:]] + [at(dp=t) for t in (x_peer, y_peer, c_peer)]
+    barrier = pltpu.get_barrier_semaphore()
+    for target in targets:
+        pl.semaphore_signal(barrier, inc=1, device_id=target, device_id_type=pl.DeviceIdType.MESH)
+    pl.semaphore_wait(barrier, len(targets))
+
+    def copy(k, kind, src, dst, target):
+        return pltpu.make_async_remote_copy(
+            src_ref=src,
+            dst_ref=dst,
+            send_sem=sem_s.at[k, kind],
+            recv_sem=sem_r.at[k, kind],
+            device_id=target,
+            device_id_type=pl.DeviceIdType.MESH,
+        )
+
+    def slot(k, c, where, low=None, high=None):
+        m, j, r0, r1 = chunks[k]
+        return land.at[m, j - 1, c, where, pl.ds(r0 if low is None else low, (r1 if high is None else high) - (r0 if low is None else low))]
+
+    def middle_row(k):
+        m, j, r0, r1 = chunks[k]
+        half = (r1 - r0) // 2
+        return r0 + (half + 7 if k % 2 else half) // 8 * 8
+
+    def over_z(k):
+        m, j, r0, r1 = chunks[k]
+        return copy(k, 0, mine_ref.at[m, pl.ds(r0, r1 - r0)], slot(k, core, spot), at(tensor=z_peer[j]))
+
+    def over_x(k):
+        return copy(k, 1, slot(k, core, spot), slot(k, core, spot), at(dp=x_peer))
+
+    def over_y(k):
+        return copy(k, 2, slot(k, core, spot), slot(k, core, spot), at(dp=y_peer))
+
+    def on_x(k):
+        part = slot(k, core, y_spot, None, middle_row(k))
+        return copy(k, 3, part, part, at(dp=x_peer))
+
+    def on_y(k):
+        part = slot(k, core, x_spot, middle_row(k), None)
+        return copy(k, 4, part, part, at(dp=y_peer))
+
+    def swap(k):
+        m, j, r0, r1 = chunks[k]
+        part = land.at[m, j - 1, core, :, pl.ds(r0, r1 - r0)]
+        return copy(k, 5, part, part, at(dp=c_peer))
+
+    bias_copies = [
+        pltpu.make_async_remote_copy(
+            src_ref=bias_ref,
+            dst_ref=biases_ref.at[j],
+            send_sem=bias_s.at[j],
+            recv_sem=bias_r.at[j],
+            device_id=at(tensor=z_peer[j]),
+            device_id_type=pl.DeviceIdType.MESH,
+        )
+        for j in (1, 2, 3)
+    ]
+    total = len(chunks)
+    ahead = 3
+    for k in range(min(ahead, total)):
+        over_z(k).start()
+    for one in bias_copies:
+        one.start()
+    biases_ref[0] = bias_ref[...]
+    for m in range(count):
+        full_ref[m, :own] = local_ref[m]
+    done = {}
+    for tick in range(total + 3):
+        k = tick
+        if k < total:
+            over_z(k).wait_recv()
+            over_x(k).start()
+            over_y(k).start()
+            if k + ahead < total:
+                over_z(k + ahead).start()
+        k = tick - 1
+        if 0 <= k < total:
+            over_y(k).wait_recv()
+            on_x(k).start()
+            over_x(k).wait_recv()
+            on_y(k).start()
+        k = tick - 2
+        if 0 <= k < total:
+            on_x(k).wait_recv()
+            on_y(k).wait_recv()
+            swap(k).start()
+        k = tick - 3
+        if 0 <= k < total:
+            swap(k).wait_recv()
+            m, j, r0, r1 = chunks[k]
+            done[m, j] = done.get((m, j), 0) + r1 - r0
+            if done[m, j] == piece:
+                full_ref[m, j * own : (j + 1) * own] = land[m, j - 1].reshape(own, -1).astype(BF)
+    for k in range(total):
+        for make in (over_z, over_x, over_y, on_x, on_y, swap):
+            make(k).wait_send()
+    for one in bias_copies:
+        one.wait()
+
+
+def gather(shards_, bias, dp, tp, ident):
+    count = len(shards_)
+    own, width = shards_[0].shape
+    bits = (2, 4) if dp == 8 else (2, 8)
+    piece = own // 8
+    local = jnp.stack(shards_)
+    d = lax.axis_index("dp")
+    at = 4 * (d % 2) + d // bits[0] % 2 + 2 * (d // bits[1] % 2)
+    mine = lax.dynamic_index_in_dim(local.reshape(count, 8, piece, width), at, 1, keepdims=False).astype(F32)
+    cut = (piece * 5 // 8) // 8 * 8
+    chunks = [(m, j, *span) for m in range(count) for j in range(1, tp) for span in ((0, cut), (cut, piece))]
+    total = len(chunks)
+    vm = pl.BlockSpec(memory_space=pltpu.VMEM)
     return pl.pallas_call(
-        round_kernel,
-        grid=(pl.cdiv(count, BLK),),
-        in_specs=[rows(width)],
-        out_specs=rows(width),
-        out_shape=jax.ShapeDtypeStruct(t.shape, BF),
-        compiler_params=params(1),
-        name="round_rows",
-    )(t)
-
-
-def gather(parts, extra, dp, tp):
-    own, width = parts[0].shape
-    piece = own // dp
-    mine = jnp.stack([t.reshape(dp, piece, width) for t in parts], axis=1)
-    mine = lax.dynamic_index_in_dim(mine, lax.axis_index("dp"), 0, keepdims=False).astype(F32)
-    mine = mine.reshape(len(parts) * piece, width)
-    if extra is not None:
-        mine = jnp.concatenate([mine, extra], axis=0)
-    full = lax.all_gather(mine, ("tensor", "dp"))
-    full = full.reshape(tp, dp, -1, width)
-    vecs = full[:, 0, len(parts) * piece :]
-    full = round_rows(full.reshape(-1, width)).reshape(full.shape)
-    twice = jnp.concatenate([full, full], axis=0)
-    full = lax.dynamic_slice_in_dim(twice, lax.axis_index("tensor"), tp, 0)
-    count = len(parts) * piece
-    body = full[:, :, :count].reshape(tp, dp, len(parts), piece, width)
-    wholes = [body[:, :, m].reshape(tp * own, width) for m in range(len(parts))]
-    vecs = jnp.concatenate([vecs, vecs], axis=0)
-    return wholes, lax.dynamic_slice_in_dim(vecs, lax.axis_index("tensor"), tp, 0)
+        functools.partial(gather_kernel, bits, chunks, count),
+        in_specs=[vm] * 3,
+        out_specs=[vm] * 2,
+        out_shape=[
+            jax.ShapeDtypeStruct((count, tp * own, width), BF),
+            jax.ShapeDtypeStruct((tp,) + bias.shape, F32),
+        ],
+        scratch_shapes=[
+            pltpu.VMEM((count, tp - 1, 2, 4, piece, width), F32),
+            pltpu.SemaphoreType.DMA((total, 6)),
+            pltpu.SemaphoreType.DMA((total, 6)),
+            pltpu.SemaphoreType.DMA((tp,)),
+            pltpu.SemaphoreType.DMA((tp,)),
+        ],
+        compiler_params=pltpu.CompilerParams(
+            collective_id=ident, has_side_effects=True, vmem_limit_bytes=VMEM_MAX
+        ),
+        cost_estimate=pl.CostEstimate(flops=0, bytes_accessed=6 * count * tp * own * width, transcendentals=0),
+        name="gather_weights",
+    )(mine, local, bias)
 
 
 def shards(dp, tp, x, g1, c1, wq, bq, wk, wv, bv, wo, bo, g2, c2, w1, b1, w2, b2, seg, valid, cot):
@@ -461,11 +581,10 @@
     def line(t):
         return t.reshape(1, -1)
 
-    biases = jnp.concatenate([bq, bv, b1]).reshape(3, own)
-    extra = jnp.zeros((8, width), F32).at[:3, :own].set(biases)
-    (fq, fk, fv), more = gather([wq.T, wk.T, wv.T], extra, dp, tp)
-    (fo, f1, f2), _ = gather([wo, w1.T, w2], None, dp, tp)
-    abq, abv, ab1 = (line(more[:, r, :own]) for r in range(3))
+    bias = jnp.zeros((8, -(-own // LANES) * LANES), F32).at[:3, :own].set(jnp.stack([bq, bv, b1]))
+    full, biases = gather([wq.T, wk.T, wv.T, wo, w1.T, w2], bias, dp, tp, 0)
+    fq, fk, fv, fo, f1, f2 = (full[m] for m in range(6))
+    abq, abv, ab1 = (line(biases[:, r, :own]) for r in range(3))
 
     normed1, q, k, v = project(x, line(g1), line(c1), fq, fk, fv, abq, abv)
     mixed, lse = attend(q, k, v, seg)

time: 672 us -> 560 us (0.83)
  waiting for transfers between devices: 324 us -> 80.2 us
  Pallas kernels: 230 us -> 361 us
  local copies, waits for them, and re-layouts: 31.6 us -> 51.4 us
  other arithmetic: 24.3 us -> 6.4 us
    all_gather x2 -> x0, waiting for transfers between devices: 246 us -> none  [gather(): full = lax.all_gather(mine, ('tensor', 'dp'))]
    pallas_call x2 -> x1, Pallas kernels: 32.1 us -> 158 us  [gather(): pl.pallas_call(functools.partial(gather_kernel, bits, chunks, count), in_...]
    concatenate x4 -> x0, other arithmetic: 16.6 us -> none  [the longest x1 14.8 us: gather(): twice = jnp.concatenate([full, full], axis=0)]
    squeeze x0 -> x1, local copies, waits for them, and re-layouts: none -> 14.5 us  [shards(): fq, fk, fv, fo, f1, f2 = (full[m] for m in range(6))]
    unnamed x41 -> x60, local copies, waits for them, and re-layouts: 11.9 us -> 24.3 us
    slice x5 -> x1, local copies, waits for them, and re-layouts: 12 us -> 0.97 us  [shards(): abq, abv, ab1 = (line(biases[:, r, :own]) for r in range(3))]
  transfers between devices with their start and end apart: 3 -> 1, of which waited for: 3 -> 1; matrix products, arithmetic and copies ran while one was open for 2% -> 1% of each run, Pallas kernels for 7% -> 6%
where the time goes in v2:
time: 560 us; the launch traced here: 555 us
  Pallas kernels  361 us (64%)
  waiting for transfers between devices  80.2 us (14%)
  local copies, waits for them, and re-layouts  51.4 us (9%)
  blocking collectives  24.4 us (4%)
  matrix products  16.8 us (3%)
  between operations  14.6 us (3%)
  other arithmetic  6.4 us (1%)
    pallas_call x1, Pallas kernels, gather(): pl.pallas_call(functools.partial(gather_kernel, bits, chunks, count), in_...  158 us
    psum x1, waiting for transfers between devices, shards(): mats = lax.psum((gq, gk, gv), 'dp')  80.2 us
    pallas_call x1, Pallas kernels, middle(): pl.pallas_call(functools.partial(middle_kernel, own), grid=(n,), in_specs...  67.6 us
    pallas_call x1, Pallas kernels, attend_back(): pl.pallas_call(attend_back_kernel, grid_spec=pltpu.PrefetchScalarGridSpec...  46.4 us
    pallas_call x1, Pallas kernels, finish(): pl.pallas_call(finish_kernel, grid=(tokens // BLK,), in_specs=[rows(inner...  33 us
    pallas_call x1, Pallas kernels, project(): pl.pallas_call(project_kernel, grid=(tokens // BLK,), in_specs=[rows(widt...  29.6 us
    pallas_call x1, Pallas kernels, attend(): pl.pallas_call(attend_kernel, grid_spec=pltpu.PrefetchScalarGridSpec(num_...  26.8 us
    psum x1, blocking collectives, shards(): lax.psum((vec[0], vec[1, :own], vec[2], vec[3], vec[4], last[0], last[1],...  24.4 us
  transfers between devices with their start and end apart: 1, of which 1 were waited for; matrix products, arithmetic and copies ran while one was open for 1% of the time, Pallas kernels for 6%

profile of v2, /device:TPU:0, one launch (start us, length us, event | category | flops | bytes accessed | tf_op | source)
XLA Modules:
  0.0 554.9 jit_solution(18127970026924349032)
XLA Ops:
  7.3 2.2 bitcast_dynamic-update-slice_fusion.3
  9.6 2.1 constant_dynamic-update-slice_fusion.5
  13.7 2.2 bitcast_dynamic-update-slice_fusion.2
  24.4 2.2 bitcast_convert_fusion.mine_ref
  27.2 157.7 %gather_weights.1 = (bf16[6,1280,1280]{2,1,0:T(8,128)(2,1)}, f32[4,8,384]{2,1,0:T(8,128)}) custom-call(f32[6,40,1280]{2,1,0:T(8,128)} %bitcast_convert_fusion.mine_ref, bf16[6,320,1280]{2,1,0:T(8,128)(2,1)} %bitcast_dynamic-update-slice_fusion.4.local_ref, f32[8,384]{1,0:T(8,128)} %select_maximum_fusion.bias_ref), custom_call_target="tpu_custom_call" | custom-call | bytes 58982400 | tf_op jit(solution)/shard_map/gather_weights/pallas_call | solution.py:553
  185.0 14.5 %slice_bitcast_fusion = (bf16[1280,1280]{1,0:T(8,128)(2,1)}, bf16[1280,1280]{1,0:T(8,128)(2,1)}, bf16[1280,1280]{1,0:T(8,128)(2,1)}, bf16[1280,1280]{1,0:T(8,128...) fusion(bf16[6,1280,1280]{2,1,0:T(8,128)(2,1)} %get-tuple-element.51), kind=kLoop, calls=%fused_computation | loop fusion | bytes 39321600 | tf_op jit(solution)/shard_map/squeeze | solution.py:586
  199.5 1.0 slice_reduce_fusion
  207.3 29.6 %project.1 = (bf16[2048,1280]{1,0:T(8,128)(2,1)}, bf16[2048,1280]{1,0:T(8,128)(2,1)}, bf16[2048,1280]{1,0:T(8,128)(2,1)}, bf16[2048,1280]{1,0:T(8,128)(2,1)}) custom-call(bf16[2048,1280]{1,0:T(8,128)(2,1)} %x_ref.5, f32[1,1280]{1,0:T(1,128)} %reshape.112.g_ref, f32[1,1280]{1,0:T(1,128)} %reshape.113.c_ref, bf16[1280,1280]{1,0:T(8,128)(2,1)} %get-tuple-element.119.wq_ref, ...), custom_call_target="tpu_custom_call" | custom-call | flops 20132659200 | bytes 36044800 | tf_op jit(solution)/shard_map/project/pallas_call | solution.py:81
  237.0 26.8 %attend.1 = (bf16[2048,1280]{1,0:T(8,128)(2,1)}, f32[2048,128]{1,0:T(8,128)}) custom-call(s32[2,1024]{1,0:T(2,128)} %seg_s.3, bf16[2048,1280]{1,0:T(8,128)(2,1)} %get-tuple-element.53.q_ref, bf16[2048,1280]{1,0:T(8,128)(2,1)} %get-tuple-element.54.k_ref, bf16[2048,1280]{1,0:T(8,128)(2,1)} %get-tuple-element.55.v_ref, s32[2,1,1024]{2,1,0:T(1,128)} %reshape.114.seg_ref), custom_call_target="tpu_custom_call" | custom-call | flops 21474836480 | bytes 20971520 | tf_op jit(solution)/shard_map/attend/pallas_call | solution.py:177
  263.8 67.6 %middle.1 = (bf16[2048,1280]{1,0:T(8,128)(2,1)}, f32[2048,1280]{1,0:T(8,128)}, bf16[2048,1280]{1,0:T(8,128)(2,1)}, f32[320,1280]{1,0:T(8,128)}, f32[320,1280]{1,...) custom-call(bf16[2048,1280]{1,0:T(8,128)(2,1)} %get-tuple-element.56.m_ref.o_ref, ...), custom_call_target="tpu_custom_call" | custom-call | flops 45298483200 | bytes 46530560 | tf_op jit(solution)/shard_map/middle/pallas_call | solution.py:359
  331.4 46.4 %attend_back.1 = (bf16[2048,1280]{1,0:T(8,128)(2,1)}, bf16[2048,1280]{1,0:T(8,128)(2,1)}, bf16[2048,1280]{1,0:T(8,128)(2,1)}) custom-call(s32[2,1024]{1,0:T(2,128)} %seg_s.3, bf16[2048,1280]{1,0:T(8,128)(2,1)} %get-tuple-element.53.q_ref, bf16[2048,1280]{1,0:T(8,128)(2,1)} %get-tuple-element.58.do_ref, bf16[2048,1280]{1,0:T(8,128)(2,1)} %get-tuple-element.56.m_ref.o_ref, ...), custom_call_target="tpu_custom_call" | custom-call | flops 53687091200 | bytes 41943040 | tf_op jit(solution)/shard_map/attend_back/pallas_call | solution.py:275
  377.8 6.2 %fusion.2 = f32[1280,320]{0,1:T(8,128)} fusion(bf16[2048,1280]{1,0:T(8,128)(2,1)} %get-tuple-element.66, bf16[2048,1280]{1,0:T(8,128)(2,1)} %get-tuple-element.62.dv_ref), kind=kOutput, calls=%fused_computation.10 | convolution fusion | flops 1677721600 | bytes 8454144 | tf_op jit(solution)/shard_map/dot_general | solution.py:34
  383.9 6.1 %fusion = f32[1280,320]{0,1:T(8,128)} fusion(bf16[2048,1280]{1,0:T(8,128)(2,1)} %get-tuple-element.66, bf16[2048,1280]{1,0:T(8,128)(2,1)} %get-tuple-element.61.dk_ref), kind=kOutput, calls=%fused_computation.8 | convolution fusion | flops 1677721600 | bytes 8454144 | tf_op jit(solution)/shard_map/dot_general | solution.py:34
  390.1 4.6 fusion.4
  394.7 33.0 %finish.1 = (f32[2048,1280]{1,0:T(8,128)}, f32[2,8,1280]{2,1,0:T(8,128)}) custom-call(bf16[2048,1280]{1,0:T(8,128)(2,1)} %get-tuple-element.60.dq_ref, bf16[2048,1280]{1,0:T(8,128)(2,1)} %get-tuple-element.61.dk_ref, bf16[2048,1280]{1,0:T(8,128)(2,1)} %get-tuple-element.62.dv_ref, bf16[2048,1280]{1,0:T(8,128)(2,1)} %x_ref.5, ...), custom_call_target="tpu_custom_call" | custom-call | flops 20132659200 | bytes 51773440 | tf_op jit(solution)/shard_map/finish/pallas_call | solution.py:404
  430.5 2.5 convert_reduce_fusion
  432.9 24.4 %all-reduce.1 = (f32[1280]{0:T(1024)}, f32[1280]{0:T(1024)}, f32[320]{0:T(512)}, f32[320]{0:T(512)}, f32[1280]{0:T(1024)}, /*index=5*/f32[1280]{0:T(1024)}, f32[1280]{0:T(1024)}, f32[320]{0:T(512)}, f32[1280]{0:T(1024)}) all-reduce(f32[1280]{0:T(1024)S(1)} %get-tuple-element.122, ...), channel_id=1, replica_groups=mesh['dp'=8,'tensor'=4] {'dp'}, use_global_device_ids=true, to_apply=%region_1.2 | all-reduce | flops 8640 | bytes 69120 | tf_op jit(solution)/shard_map/psum | solution.py:609
  457.3 80.2 %all-reduce.5.cloned.1.call-done = (f32[1280,320]{0,1:T(8,128)}, f32[1280,320]{0,1:T(8,128)}, f32[1280,320]{0,1:T(8,128)}, f32[320,1280]{1,0:T(8,128)}, f32[1280,320]{0,1:T(8,128)}, /*index=5*/f32[320,1280]{1,0:T(8,128)}) async-done(((f32[1280,320]{0,1:T(8,128)}, f32[1280,320]{0,1:T(8,128)}, f32[1280,320]{0,1:T(8,128)}, f32[320,1280]{1,0:T(8,128)}, f32[1280,320]{0,1:T(8,128)}, ...) | async-done | bytes 9830416 | tf_op jit(solution)/shard_map/psum | solution.py:608
  537.5 2.8 copy.71
  540.3 2.8 copy.72
  543.1 1.2 copy.73
  544.3 1.2 copy.74
  545.5 1.2 copy.75
  546.6 1.2 copy.76
  (81 shorter events, 20.9 us)
Async XLA Ops:
  7.2 8.7 %copy-start = (bf16[1280,320]{0,1:T(8,128)(2,1)S(1)}, bf16[1280,320]{0,1:T(8,128)(2,1)}, u32[]{:S(2)}) copy-start(bf16[1280,320]{0,1:T(8,128)(2,1)} %param.26) | copy-start | bytes 2457604
  7.2 9.6 %copy-start.1 = (bf16[1280,320]{0,1:T(8,128)(2,1)S(1)}, bf16[1280,320]{0,1:T(8,128)(2,1)}, u32[]{:S(2)}) copy-start(bf16[1280,320]{0,1:T(8,128)(2,1)} %param.27) | copy-start | bytes 2457604
  7.2 530.2 %all-reduce.5.cloned.1.call-start = ((), (), s32[]{:S(2)}) async-start(), calls=%async_computation | async-start | bytes 19660800 | tf_op jit(solution)/shard_map/psum | solution.py:608
  7.3 11.4 %copy-start.2 = (bf16[320,1280]{1,0:T(8,128)(2,1)S(1)}, bf16[320,1280]{1,0:T(8,128)(2,1)}, u32[]{:S(2)}) copy-start(bf16[320,1280]{1,0:T(8,128)(2,1)} %param.29) | copy-start | bytes 2457604
  13.7 6.9 %copy-start.3 = (bf16[1280,320]{0,1:T(8,128)(2,1)S(1)}, bf16[1280,320]{0,1:T(8,128)(2,1)}, u32[]{:S(2)}) copy-start(bf16[1280,320]{0,1:T(8,128)(2,1)} %param.33) | copy-start | bytes 2457604
  16.8 5.7 %copy-start.4 = (bf16[320,1280]{1,0:T(8,128)(2,1)S(1)}, bf16[320,1280]{1,0:T(8,128)(2,1)}, u32[]{:S(2)}) copy-start(bf16[320,1280]{1,0:T(8,128)(2,1)} %param.35) | copy-start | bytes 2457604
  184.9 17.0 %copy-start.13 = (f32[1280]{0:T(1024)S(1)}, f32[1280]{0:T(1024)}, u32[]{:S(2)}) copy-start(f32[1280]{0:T(1024)} %param.22) | copy-start | bytes 15364
  184.9 17.6 %copy-start.14 = (f32[1280]{0:T(1024)S(1)}, f32[1280]{0:T(1024)}, u32[]{:S(2)}) copy-start(f32[1280]{0:T(1024)} %param.23) | copy-start | bytes 15364
  184.9 18.1 %copy-start.12 = (s32[2,1024]{1,0:T(2,128)S(1)}, s32[2,1024]{1,0:T(2,128)}, u32[]{:S(2)}) copy-start(s32[2,1024]{1,0:T(2,128)} %seg_s.3) | copy-start | bytes 24580
  184.9 19.4 %copy-start.10 = (s32[2,1024]{1,0:T(2,128)S(1)}, s32[2,1024]{1,0:T(2,128)}, u32[]{:S(2)}) copy-start(s32[2,1024]{1,0:T(2,128)} %param.38) | copy-start | bytes 24580
  184.9 20.0 %copy-start.15 = (f32[1280]{0:T(1024)S(1)}, f32[1280]{0:T(1024)}, u32[]{:S(2)}) copy-start(f32[1280]{0:T(1024)} %param.30) | copy-start | bytes 15364
  184.9 20.6 %copy-start.16 = (f32[1280]{0:T(1024)S(1)}, f32[1280]{0:T(1024)}, u32[]{:S(2)}) copy-start(f32[1280]{0:T(1024)} %param.31) | copy-start | bytes 15364
  184.9 21.2 %copy-start.17 = (f32[1280]{0:T(1024)S(1)}, f32[1280]{0:T(1024)}, u32[]{:S(2)}) copy-start(f32[1280]{0:T(1024)} %param.32) | copy-start | bytes 15364
  185.0 21.8 %copy-start.18 = (f32[1280]{0:T(1024)S(1)}, f32[1280]{0:T(1024)}, u32[]{:S(2)}) copy-start(f32[1280]{0:T(1024)} %param.36) | copy-start | bytes 15364
  377.8 12.3 %slice-start = ((s8[5242880]{0:T(1024)(128)(4,1)}), s8[4194304]{0:T(1024)(128)(4,1)S(1)}, s32[]{:S(2)}) async-start(s8[5242880]{0:T(1024)(128)(4,1)} %bitcast.66), calls=%async_computation.1 | async-start | bytes 8388608
  383.9 6.1 %slice-start.1 = ((s8[5242880]{0:T(1024)(128)(4,1)}), s8[1048576]{0:T(1024)(128)(4,1)S(1)}, s32[]{:S(2)}) async-start(s8[5242880]{0:T(1024)(128)(4,1)} %bitcast.66), calls=%async_computation.2 | async-start | bytes 2097152
  394.6 34.0 %copy-start.9 = (f32[5,8,1280]{2,1,0:T(8,128)S(1)}, f32[5,8,1280]{2,1,0:T(8,128)}, u32[]{:S(2)}) copy-start(f32[5,8,1280]{2,1,0:T(8,128)} %get-tuple-element.68) | copy-start | bytes 614404
  394.7 34.9 %copy-start.11 = (s32[2,1024]{1,0:T(2,128)S(1)}, s32[2,1024]{1,0:T(2,128)}, u32[]{:S(2)}) copy-start(s32[2,1024]{1,0:T(2,128)} %param.38) | copy-start | bytes 24580
  537.5 5.7 %copy-start.8 = (f32[1280,320]{0,1:T(8,128)S(1)}, f32[1280,320]{0,1:T(8,128)}, u32[]{:S(2)}) copy-start(f32[1280,320]{0,1:T(8,128)} %get-tuple-element.131) | copy-start | bytes 4915204
  537.5 6.8 %copy-start.7 = (f32[320,1280]{1,0:T(8,128)S(1)}, f32[320,1280]{1,0:T(8,128)}, u32[]{:S(2)}) copy-start(f32[320,1280]{1,0:T(8,128)} %get-tuple-element.133) | copy-start | bytes 4915204
  540.3 5.2 copy-start.6
  543.1 3.5 copy-start.5
Sparse Core Ops, SparseCore 0:
  394.8 142.6 all-reduce.4

commit v3 on v1

v3 whole, which is shorter than its diff:
```python
import functools
import math

import jax
import jax.numpy as jnp
from jax import lax
from jax.experimental import pallas as pl
from jax.experimental.pallas import tpu as pltpu
from jax.sharding import PartitionSpec as P

HEAD_DIM = 160
MAX_DOC = 512
EPS = 1e-05
NEG = -1e30
BLK = 256
WIN = 256
LANES = 128
SCALE = 1.0 / math.sqrt(HEAD_DIM)
LOG2E = 1.0 / math.log(2.0)
BF = jnp.bfloat16
F32 = jnp.float32
VMEM_MAX = 60 << 20


def nn(a, b):
    return lax.dot_general(a, b, (((1,), (0,)), ((), ())), preferred_element_type=F32)


def nt(a, b):
    return lax.dot_general(a, b, (((1,), (1,)), ((), ())), preferred_element_type=F32)


def tn(a, b):
    return lax.dot_general(a, b, (((0,), (0,)), ((), ())), preferred_element_type=F32)


def whole(shape):
    return pl.BlockSpec(shape, lambda *_: (0,) * len(shape), pipeline_mode=pl.Buffered(1))


def held(shape):
    return pl.BlockSpec(shape, lambda *_: (0,) * len(shape))


def rows(width):
    return pl.BlockSpec((BLK, width), lambda i: (i, 0))


def column_of(row):
    n = row.shape[1]
    eye = lax.broadcasted_iota(jnp.int32, (n, n), 0) == lax.broadcasted_iota(jnp.int32, (n, n), 1)
    return jnp.sum(jnp.where(eye, row, jnp.zeros_like(row)), axis=1, keepdims=True)


def fold8(t):
    return jnp.sum(t.reshape(t.shape[0] // 8, 8, t.shape[1]), axis=0)


def params(grid, vmem=VMEM_MAX):
    return pltpu.CompilerParams(dimension_semantics=("arbitrary",) * grid, vmem_limit_bytes=vmem)


def hosting(grid, ident):
    return pltpu.CompilerParams(
        dimension_semantics=("arbitrary",) * grid,
        vmem_limit_bytes=VMEM_MAX,
        collective_id=ident,
        has_side_effects=True,
    )


def sibling(index, bit):
    return index + bit - 2 * bit * (index // bit % 2)


class Place:
    def __init__(self, bits):
        self.d, self.z = lax.axis_index("dp"), lax.axis_index("tensor")
        self.core = self.d % 2
        self.a, self.b = (self.d // bit % 2 for bit in bits)
        self.spot = self.a + 2 * self.b
        self.on_core = {"dp": sibling(self.d, 1), "tensor": self.z}
        self.on_a, self.on_b = ({"dp": sibling(self.d, bit), "tensor": self.z} for bit in bits)
        peers = (None, sibling(self.z, 1), sibling(self.z, 2), sibling(sibling(self.z, 1), 2))
        self.on_z = [None] + [{"dp": self.d, "tensor": peer} for peer in peers[1:]]

    def plane(self):
        return [{"dp": (self.d + step) % 8, "tensor": self.z} for step in range(1, 8)]


def greet(targets):
    barrier = pltpu.get_barrier_semaphore()
    for target in targets:
        pl.semaphore_signal(barrier, inc=1, device_id=target, device_id_type=pl.DeviceIdType.MESH)
    pl.semaphore_wait(barrier, len(targets))


def send(src, dst, sems, at, target):
    return pltpu.make_async_remote_copy(
        src_ref=src,
        dst_ref=dst,
        send_sem=sems[0].at[at],
        recv_sem=sems[1].at[at],
        device_id=target,
        device_id_type=pl.DeviceIdType.MESH,
    )


def bits_of(dp):
    return (2, 4) if dp == 8 else (2, 8)


def chunks_of(count, tp, piece):
    cut = (piece * 5 // 8) // 8 * 8
    return [(m, j, *span) for m in range(count) for j in range(1, tp) for span in ((0, cut), (cut, piece))]


AHEAD = 3


class Gather:
    def __init__(self, place, chunks, mine, local, full, land, sems):
        self.place, self.chunks, self.mine, self.local, self.full, self.land, self.sems = (
            place, chunks, mine, local, full, land, sems
        )
        self.ticks = len(chunks) + 3
        self.got = {}

    def slot(self, k, where, low=None, high=None):
        m, j, r0, r1 = self.chunks[k]
        low, high = (r0 if low is None else low), (r1 if high is None else high)
        return self.land.at[m, j - 1, self.place.core, where, pl.ds(low, high - low)]

    def middle(self, k):
        _, _, r0, r1 = self.chunks[k]
        half = (r1 - r0) // 2
        return r0 + (half + 7 if k % 2 else half) // 8 * 8

    def over_z(self, k):
        m, j, r0, r1 = self.chunks[k]
        here = self.slot(k, self.place.spot)
        return send(self.mine.at[m, pl.ds(r0, r1 - r0)], here, self.sems, (k, 0), self.place.on_z[j])

    def over_a(self, k):
        here = self.slot(k, self.place.spot)
        return send(here, here, self.sems, (k, 1), self.place.on_a)

    def over_b(self, k):
        here = self.slot(k, self.place.spot)
        return send(here, here, self.sems, (k, 2), self.place.on_b)

    def on_a(self, k):
        part = self.slot(k, sibling(self.place.spot, 2), None, self.middle(k))
        return send(part, part, self.sems, (k, 3), self.place.on_a)

    def on_b(self, k):
        part = self.slot(k, sibling(self.place.spot, 1), self.middle(k), None)
        return send(part, part, self.sems, (k, 4), self.place.on_b)

    def swap(self, k):
        m, j, r0, r1 = self.chunks[k]
        part = self.land.at[m, j - 1, self.place.core, :, pl.ds(r0, r1 - r0)]
        return send(part, part, self.sems, (k, 5), self.place.on_core)

    def begin(self):
        place = self.place
        greet(place.on_z[1:] + [place.on_a, place.on_b, place.on_core])
        for k in range(min(AHEAD, len(self.chunks))):
            self.over_z(k).start()
        for full, local in zip(self.full, self.local):
            full[: local.shape[0]] = local[...]

    def tick(self, t):
        total = len(self.chunks)
        if 0 <= t < total:
            self.over_z(t).wait_recv()
            self.over_a(t).start()
            self.over_b(t).start()
            if t + AHEAD < total:
                self.over_z(t + AHEAD).start()
        k = t - 1
        if 0 <= k < total:
            self.over_b(k).wait_recv()
            self.on_a(k).start()
            self.over_a(k).wait_recv()
            self.on_b(k).start()
        k = t - 2
        if 0 <= k < total:
            self.on_a(k).wait_recv()
            self.on_b(k).wait_recv()
            self.swap(k).start()
        k = t - 3
        if 0 <= k < total:
            self.swap(k).wait_recv()
            m, j, r0, r1 = self.chunks[k]
            piece = self.land.shape[4]
            self.got[m, j] = self.got.get((m, j), 0) + r1 - r0
            if self.got[m, j] == piece:
                own = 8 * piece
                self.full[m][j * own : (j + 1) * own] = self.land[m, j - 1].reshape(own, -1).astype(BF)

    def end(self):
        for k in range(len(self.chunks)):
            for make in (self.over_z, self.over_a, self.over_b, self.on_a, self.on_b, self.swap):
                make(k).wait_send()


def gather_scratch(count, tp, piece, width):
    total = len(chunks_of(count, tp, piece))
    return [
        pltpu.VMEM((count, tp - 1, 2, 4, piece, width), F32),
        pltpu.SemaphoreType.DMA((total, 6)),
        pltpu.SemaphoreType.DMA((total, 6)),
    ]


class Reduce:
    def __init__(self, place, part, scratch, publish):
        self.place, self.part, self.publish = place, part, publish
        self.out, self.half, self.from_core, self.first, self.second, *self.sems = scratch
        self.count, self.own, self.width = part.shape
        self.ticks = self.count + 6

    def greet(self):
        return [self.place.on_a, self.place.on_b, self.place.on_core]

    def ways(self):
        place = self.place
        return (
            (0, place.a, place.on_a, place.b, place.on_b),
            (1, place.b, place.on_b, place.a, place.on_a),
        )

    def rows_of(self, size, index, count):
        return pl.ds(pl.multiple_of(size * index, 8), count)

    def out_rows(self, way, bit):
        quarter = self.own // 8
        return self.rows_of(quarter, 4 * self.place.core + 2 * way + bit, quarter)

    def copies(self, m, stage):
        place, own = self.place, self.own
        quarter, lanes = own // 8, self.width // 2
        if stage == 0:
            src = self.part.at[m, self.rows_of(own // 2, 1 - place.core, own // 2)]
            return [send(src, self.from_core.at[m], self.sems, (m, 0, 0), place.on_core)]
        if stage == 5:
            rows_ = self.out.at[m, self.rows_of(own // 2, place.core, own // 2)]
            return [send(rows_, rows_, self.sems, (m, 5, 0), place.on_core)]
        made = []
        for way, bit, peer, bit2, peer2 in self.ways():
            columns = pl.ds(pl.multiple_of(lanes * bit2, LANES), lanes)
            others = pl.ds(pl.multiple_of(lanes * (1 - bit2), LANES), lanes)
            if stage == 1:
                src, dst, to = self.half.at[m, self.rows_of(quarter, 2 * way + 1 - bit, quarter)], self.first.at[m, way], peer
            elif stage == 2:
                src = self.half.at[m, self.rows_of(quarter, 2 * way + bit, quarter), others]
                dst, to = self.second.at[m, way], peer2
            elif stage == 3:
                src = dst = self.out.at[m, self.out_rows(way, bit), columns]
                to = peer2
            else:
                src = dst = self.out.at[m, self.out_rows(way, bit)]
                to = peer
            made.append(send(src, dst, self.sems, (m, stage, way), to))
        return made

    def step(self, m, stage):
        if stage >= 1:
            for one in self.copies(m, stage - 1):
                one.wait_recv()
        place, own = self.place, self.own
        quarter, lanes = own // 8, self.width // 2
        if stage == 1:
            self.half[m] = self.part[m, self.rows_of(own // 2, place.core, own // 2)] + self.from_core[m]
        for way, bit, _, bit2, _ in self.ways():
            mine = self.rows_of(quarter, 2 * way + bit, quarter)
            columns = pl.ds(pl.multiple_of(lanes * bit2, LANES), lanes)
            if stage == 2:
                self.half[m, mine] = self.half[m, mine] + self.first[m, way]
            if stage == 3:
                self.out[m, self.out_rows(way, bit), columns] = self.half[m, mine, columns] + self.second[m, way]
        if stage < 6:
            for one in self.copies(m, stage):
                one.start()
        else:
            self.publish(m, self.out[m])

    def tick(self, t):
        for m in range(self.count):
            if 0 <= t - m <= 6:
                self.step(m, t - m)

    def end(self):
        for m in range(self.count):
            for stage in range(6):
                for one in self.copies(m, stage):
                    one.wait_send()


def reduce_scratch(count, own, width):
    return [
        pltpu.VMEM((count, own, width), F32),
        pltpu.VMEM((count, own // 2, width), F32),
        pltpu.VMEM((count, own // 2, width), F32),
        pltpu.VMEM((count, 2, own // 8, width), F32),
        pltpu.VMEM((count, 2, own // 8, width // 2), F32),
        pltpu.SemaphoreType.DMA((count, 6, 2)),
        pltpu.SemaphoreType.DMA((count, 6, 2)),
    ]


def host(work, step, steps, spread_over=None):
    spread_over = spread_over or steps
    for t in range(work.ticks):
        pl.when(step == t * spread_over // work.ticks)(functools.partial(work.tick, t))
    pl.when(step == steps - 1)(work.end)


def gather_kernel(bits, chunks, count, mine, *refs):
    local, bias_ref = refs[:count], refs[count]
    full, biases_ref, land = refs[count + 1 : 2 * count + 1], refs[2 * count + 1], refs[2 * count + 2]
    sems, bias_sems = refs[2 * count + 3 : 2 * count + 5], refs[2 * count + 5 :]
    place = Place(bits)
    work = Gather(place, chunks, mine, local, full, land, sems)
    work.begin()
    vectors = [send(bias_ref, biases_ref.at[j], bias_sems, j, place.on_z[j]) for j in range(1, len(place.on_z))]
    for one in vectors:
        one.start()
    biases_ref[0] = bias_ref[...]
    for t in range(work.ticks):
        work.tick(t)
    work.end()
    for one in vectors:
        one.wait()


def slices_of(shards_, bits):
    own, width = shards_[0].shape
    piece = own // 8
    d = lax.axis_index("dp")
    at = 4 * (d % 2) + d // bits[0] % 2 + 2 * (d // bits[1] % 2)
    cut = [lax.dynamic_index_in_dim(t.reshape(8, piece, width), at, 0, keepdims=False) for t in shards_]
    return [t.astype(F32) for t in cut]


def gather(shards_, bias, dp, tp):
    count = len(shards_)
    own, width = shards_[0].shape
    bits = bits_of(dp)
    piece = own // 8
    mine = jnp.stack(slices_of(shards_, bits))
    vm = pl.BlockSpec(memory_space=pltpu.VMEM)
    return pl.pallas_call(
        functools.partial(gather_kernel, bits, chunks_of(count, tp, piece), count),
        in_specs=[vm] * (count + 2),
        out_specs=[vm] * (count + 1),
        out_shape=[jax.ShapeDtypeStruct((tp * own, width), BF)] * count + [jax.ShapeDtypeStruct((tp,) + bias.shape, F32)],
        scratch_shapes=gather_scratch(count, tp, piece, width)
        + [pltpu.SemaphoreType.DMA((tp,)), pltpu.SemaphoreType.DMA((tp,))],
        compiler_params=pltpu.CompilerParams(collective_id=0, has_side_effects=True, vmem_limit_bytes=VMEM_MAX),
        cost_estimate=pl.CostEstimate(flops=0, bytes_accessed=6 * count * tp * own * width, transcendentals=0),
        name="gather_weights",
    )(mine, *shards_, bias)


def normalize(v):
    center = v - jnp.mean(v, axis=-1, keepdims=True)
    inv = lax.rsqrt(jnp.mean(center * center, axis=-1, keepdims=True) + EPS)
    return center * inv, inv


def project_kernel(
    bits, steps, chunks, x_ref, g_ref, c_ref, wq_ref, wk_ref, wv_ref, bq_ref, bv_ref, mine, *refs
):
    count = mine.shape[0]
    local, refs = refs[:count], refs[count:]
    n_ref, q_ref, k_ref, v_ref, *full = refs[: 4 + count]
    land, *sems = refs[4 + count :]
    step = pl.program_id(0)
    work = Gather(Place(bits), chunks, mine, local, full, land, sems)
    pl.when(step == 0)(work.begin)
    hat, _ = normalize(x_ref[...].astype(F32))
    normed = (hat * g_ref[...] + c_ref[...]).astype(BF)
    n_ref[...] = normed
    q_ref[...] = (nt(normed, wq_ref[...]) + bq_ref[...]).astype(BF)
    k_ref[...] = nt(normed, wk_ref[...]).astype(BF)
    v_ref[...] = (nt(normed, wv_ref[...]) + bv_ref[...]).astype(BF)
    host(work, step, steps)


def project(x, g1, c1, wq, wk, wv, bq, bv, shards_, dp, tp):
    tokens, width = x.shape
    out = wq.shape[0]
    count, own = len(shards_), shards_[0].shape[0]
    bits, piece, steps = bits_of(dp), own // 8, tokens // BLK
    mine = jnp.stack(slices_of(shards_, bits))
    return pl.pallas_call(
        functools.partial(project_kernel, bits, steps, chunks_of(count, tp, piece)),
        grid=(steps,),
        in_specs=[rows(width), whole((1, width)), whole((1, width))]
        + [whole((out, width))] * 3
        + [whole((1, out))] * 2
        + [whole(mine.shape)]
        + [whole((own, width))] * count,
        out_specs=[rows(width)] + [rows(out)] * 3 + [held((tp * own, width))] * count,
        out_shape=[jax.ShapeDtypeStruct((tokens, width), BF)]
        + [jax.ShapeDtypeStruct((tokens, out), BF)] * 3
        + [jax.ShapeDtypeStruct((tp * own, width), BF)] * count,
        scratch_shapes=gather_scratch(count, tp, piece, width),
        compiler_params=hosting(1, 1),
        cost_estimate=pl.CostEstimate(
            flops=6 * tokens * width * out, bytes_accessed=2 * (tokens * (2 * width + 3 * out) + 3 * width * out), transcendentals=0
        ),
        name="project",
    )(x, g1, c1, wq, wk, wv, bq, bv, mine, *shards_)


HEADS_IN_GROUP = 4
GROUP = HEADS_IN_GROUP * HEAD_DIM


def window_of(head):
    low = head * HEAD_DIM
    start = low // LANES * LANES
    return start, low - start


def lane_mask(offset):
    lane = lax.broadcasted_iota(jnp.int32, (1, WIN), 1)
    return (lane >= offset) & (lane < offset + HEAD_DIM)


def spread(parts):
    tiles = [None] * (GROUP // LANES)
    for head, part in enumerate(parts):
        first = window_of(head)[0] // LANES
        for half in range(WIN // LANES):
            piece = part[:, half * LANES : (half + 1) * LANES]
            at = first + half
            tiles[at] = piece if tiles[at] is None else tiles[at] + piece
    return jnp.concatenate(tiles, axis=1)


def attend_kernel(bits, steps, chunks, q_ref, k_ref, v_ref, seg_ref, mine, *refs):
    kinds = mine.shape[0]
    local, refs = refs[:kinds], refs[kinds:]
    o_ref, lse_ref, *full = refs[: 2 + kinds]
    bias, land, *sems = refs[2 + kinds :]
    s, i = pl.program_id(0), pl.program_id(1)
    groups = q_ref.shape[1] // GROUP
    back = MAX_DOC // BLK
    count = jnp.minimum(i, back) + 1
    step = s * pl.num_programs(1) + i
    work = Gather(Place(bits), chunks, mine, local, full, land, sems)
    pl.when(step == 0)(work.begin)
    seg_col = column_of(seg_ref[0, :, pl.ds(pl.multiple_of(i * BLK, BLK), BLK)])

    def body(blocks):
        keys = blocks * BLK
        start = pl.multiple_of((i + 1 - blocks) * BLK, BLK)
        row = i * BLK + lax.broadcasted_iota(jnp.int32, (BLK, keys), 0)
        col = start + lax.broadcasted_iota(jnp.int32, (BLK, keys), 1)
        allowed = (row >= col) & (seg_col == seg_ref[0, :, pl.ds(start, keys)])
        bias[:, :keys] = jnp.where(allowed, 0.0, NEG)

        def group(gi, _):
            parts = []
            lse = lse_ref[...]
            head_lane = lax.broadcasted_iota(jnp.int32, (1, LANES), 1)
            for h in range(HEADS_IN_GROUP):
                at, off = window_of(h)
                lanes = pl.ds(pl.multiple_of(gi * GROUP + at, LANES), WIN)
                mask = lane_mask(off)
                q = q_ref[:, lanes]
                q = jnp.where(mask, q, jnp.zeros_like(q))
                t = nt(q, k_ref[pl.ds(start, keys), lanes]) * (SCALE * LOG2E) + bias[:, :keys]
                top = jnp.max(t, axis=1, keepdims=True)
                p = jnp.exp2(t - top)
                total = jnp.sum(p, axis=1, keepdims=True)
                o = nn(p.astype(BF), v_ref[pl.ds(start, keys), lanes])
                parts.append(jnp.where(mask, o * (1.0 / total), 0.0))
                lse = jnp.where(head_lane == gi * HEADS_IN_GROUP + h, top + jnp.log2(total), lse)
            lse_ref[...] = lse
            o_ref[:, pl.ds(pl.multiple_of(gi * GROUP, LANES), GROUP)] = spread(parts).astype(BF)
            return 0

        lax.fori_loop(0, groups, group, 0)

    lse_ref[...] = jnp.zeros_like(lse_ref)
    for blocks in range(1, back + 2):
        pl.when(count == blocks)(functools.partial(body, blocks))
    host(work, step, steps)


def attend(q, k, v, seg, shards_, dp, tp):
    tokens, width = q.shape
    seqs, length = seg.shape
    n = length // BLK
    count, own = len(shards_), shards_[0].shape[0]
    bits, piece = bits_of(dp), own // 8
    mine = jnp.stack(slices_of(shards_, bits))
    spec_q = pl.BlockSpec((BLK, width), lambda s, i: (s * n + i, 0))
    spec_k = pl.BlockSpec((length, width), lambda s, i: (s, 0))
    pairs = seqs * n * 2.5 * BLK * BLK * (width // HEAD_DIM)
    return pl.pallas_call(
        functools.partial(attend_kernel, bits, seqs * n, chunks_of(count, tp, piece)),
        grid=(seqs, n),
        in_specs=[spec_q, spec_k, spec_k, pl.BlockSpec((1, 1, length), lambda s, i: (s, 0, 0)), whole(mine.shape)]
        + [whole((own, shards_[0].shape[1]))] * count,
        out_specs=[spec_q, pl.BlockSpec((BLK, LANES), lambda s, i: (s * n + i, 0))]
        + [held((tp * own, shards_[0].shape[1]))] * count,
        scratch_shapes=[pltpu.VMEM((BLK, BLK + MAX_DOC), F32)]
        + gather_scratch(count, tp, piece, shards_[0].shape[1]),
        out_shape=[jax.ShapeDtypeStruct((tokens, width), BF), jax.ShapeDtypeStruct((tokens, LANES), F32)]
        + [jax.ShapeDtypeStruct((tp * own, shards_[0].shape[1]), BF)] * count,
        compiler_params=hosting(2, 2),
        cost_estimate=pl.CostEstimate(
            flops=int(pairs * 8 * WIN), bytes_accessed=8 * tokens * width, transcendentals=int(pairs)
        ),
        name="attend",
    )(q, k, v, seg.reshape(seqs, 1, length), mine, *shards_)


def attend_back_kernel(
    steps, bits, q_ref, do_ref, o_ref, lse_ref, k_ref, v_ref, seg_ref, part_ref, dq_ref, dk_ref, dv_ref, go_ref, g1_ref, g2_ref,
    bias, dq_acc, lse_t, delta_t, *reduce_refs,
):
    s, j = pl.program_id(0), pl.program_id(1)
    n = pl.num_programs(1)
    length, width = q_ref.shape
    groups = width // GROUP
    ahead = MAX_DOC // BLK

    def publish(m, total):
        (go_ref, g1_ref, g2_ref)[m][...] = total.T if m == 1 else total

    if bits is not None:
        work = Reduce(Place(bits), part_ref, reduce_refs, publish)

    @pl.when(j == 0)
    def _():
        dq_acc[...] = jnp.zeros_like(dq_acc)
        head = lax.broadcasted_iota(jnp.int32, (16, width), 0)
        lane = lax.broadcasted_iota(jnp.int32, (16, width), 1)
        pick = jnp.where((lane >= head * HEAD_DIM) & (lane < (head + 1) * HEAD_DIM), 1.0, 0.0).astype(BF)
        for b in range(length // BLK):
            at = slice(b * BLK, (b + 1) * BLK)
            lse_t[:, at] = lse_ref[at, :].T[:16, :]
            prod = do_ref[at, :].astype(F32) * o_ref[at, :].astype(F32)
            high = prod.astype(BF)
            rest = (prod - high.astype(F32)).astype(BF)
            delta_t[:, at] = nt(pick, high) + nt(pick, rest)

    count = jnp.minimum(n - j, ahead + 1)
    start = pl.multiple_of(j * BLK, BLK)
    seg_col = column_of(seg_ref[0, :, pl.ds(start, BLK)])

    def body(blocks):
        queries = blocks * BLK
        span = pl.ds(start, queries)
        row = lax.broadcasted_iota(jnp.int32, (BLK, queries), 0)
        col = lax.broadcasted_iota(jnp.int32, (BLK, queries), 1)
        allowed = (row <= col) & (seg_col == seg_ref[0, :, span])
        bias[:, :queries] = jnp.where(allowed, 0.0, NEG)

        def group(gi, _):
            dks, dvs = [], []
            for h in range(HEADS_IN_GROUP):
                at, off = window_of(h)
                lanes = pl.ds(pl.multiple_of(gi * GROUP + at, LANES), WIN)
                mask = lane_mask(off)
                head = pl.ds(gi * HEADS_IN_GROUP + h, 1)
                k = k_ref[:, lanes]
                k = jnp.where(mask, k, jnp.zeros_like(k))
                v = v_ref[:, lanes]
                v = jnp.where(mask, v, jnp.zeros_like(v))
                q = q_ref[span, lanes]
                do = do_ref[span, lanes]
                t = nt(k, q) * (SCALE * LOG2E) + bias[:, :queries]
                p = jnp.exp2(t - lse_t[head, span])
                dvs.append(jnp.where(mask, nn(p.astype(BF), do), 0.0))
                ds = (p * (nt(v, do) - delta_t[head, span])).astype(BF)
                dks.append(jnp.where(mask, nn(ds, q), 0.0))
                dq_acc[span, lanes] += tn(ds, k)
            out = pl.ds(pl.multiple_of(gi * GROUP, LANES), GROUP)
            dk_ref[:, out] = (spread(dks) * SCALE).astype(BF)
            dv_ref[:, out] = spread(dvs).astype(BF)
            return 0

        lax.fori_loop(0, groups, group, 0)

    step = s * n + j
    if bits is not None:

        @pl.when(step == 0)
        def _():
            greet(work.greet())
            work.tick(0)

    for blocks in range(1, ahead + 2):
        pl.when(count == blocks)(functools.partial(body, blocks))

    if bits is not None:
        for t in range(1, work.ticks):
            pl.when(step == min(t - 1, steps - 1))(functools.partial(work.tick, t))
        pl.when(step == steps - 1)(work.end)
    else:
        for m in range(3):
            publish(m, part_ref[m])

    @pl.when(j == n - 1)
    def _():
        dq_ref[...] = (dq_acc[...] * SCALE).astype(BF)


def attend_back(q, k, v, seg, mixed, d_mixed, lse, parts, bits):
    tokens, width = q.shape
    seqs, length = seg.shape
    own, model = parts.shape[1:]
    n = length // BLK
    spec_k = pl.BlockSpec((BLK, width), lambda s, j: (s * n + j, 0))
    spec_q = pl.BlockSpec((length, width), lambda s, j: (s, 0))
    pairs = seqs * n * 2.5 * BLK * BLK * (width // HEAD_DIM)
    hosted = bits is not None
    turned = [(own, model), (model, own), (own, model)]
    return pl.pallas_call(
        functools.partial(attend_back_kernel, seqs * n, bits),
        grid=(seqs, n),
        in_specs=[
            spec_q,
            spec_q,
            spec_q,
            pl.BlockSpec((length, LANES), lambda s, j: (s, 0)),
            spec_k,
            spec_k,
            pl.BlockSpec((1, 1, length), lambda s, j: (s, 0, 0)),
            whole(parts.shape),
        ],
        out_specs=[spec_q, spec_k, spec_k] + [held(t) for t in turned],
        scratch_shapes=[
            pltpu.VMEM((BLK, BLK + MAX_DOC), F32),
            pltpu.VMEM((length, width), F32),
            pltpu.VMEM((16, length), F32),
            pltpu.VMEM((16, length), F32),
        ]
        + (reduce_scratch(*parts.shape) if hosted else []),
        out_shape=[jax.ShapeDtypeStruct((tokens, width), BF)] * 3 + [jax.ShapeDtypeStruct(t, F32) for t in turned],
        compiler_params=hosting(2, 3) if hosted else params(2),
        cost_estimate=pl.CostEstimate(
            flops=int(pairs * 20 * WIN), bytes_accessed=16 * tokens * width, transcendentals=int(pairs)
        ),
        name="attend_back",
    )(q, d_mixed, mixed, lse, k, v, seg.reshape(seqs, 1, length), parts)


OWN_ROW = 6


def middle_kernel(
    own, m_ref, x_ref, g_ref, w_ref, wo_ref, w1_ref, w2_ref, bo_ref, g2_ref, c2_ref, b1_ref, b2_ref,
    y_ref, dr_ref, dm_ref, part_ref, small_ref, sq_ref, vec,
):
    i = pl.program_id(0)

    @pl.when(i == 0)
    def _():
        part_ref[...] = jnp.zeros_like(part_ref)
        vec[...] = jnp.zeros_like(vec)

    mixed = m_ref[...]
    cot = g_ref[...]
    attended = nn(mixed, wo_ref[...]) + bo_ref[...]
    resid = x_ref[...].astype(F32) + attended
    hat, inv = normalize(resid)
    normed = (hat * g2_ref[...] + c2_ref[...]).astype(BF)
    pre = nt(normed, w1_ref[...]) + b1_ref[...]
    cdf = 0.5 + 0.5 * lax.erf(pre * math.sqrt(0.5))
    act = (pre * cdf).astype(BF)
    slope = cdf + pre * jnp.exp(-0.5 * pre * pre) * (1.0 / math.sqrt(2.0 * math.pi))
    branch = nn(act, w2_ref[...]) + b2_ref[...]
    output = resid + branch
    y_ref[...] = output.astype(BF)
    weight = column_of(w_ref[0])
    lane = lax.broadcasted_iota(jnp.int32, (1, LANES), 1)
    sums = jnp.zeros((1, LANES), F32)
    for at, v in enumerate((attended, branch, output)):
        one = jnp.sum(weight * jnp.sum(v * v, axis=1, keepdims=True), axis=0, keepdims=True)
        sums = jnp.where(lane == at, one, sums)
    sq_ref[...] = jnp.broadcast_to(sums, sq_ref.shape[1:])[None]

    d_pre = (nt(cot, w2_ref[...]) * slope).astype(BF)
    part_ref[2] += tn(act[:, :own], cot)
    part_ref[1] += tn(d_pre[:, :own], normed)
    d_normed = nn(d_pre, w1_ref[...])
    d_hat = d_normed * g2_ref[...]
    grad = cot.astype(F32)
    d_resid = grad + inv * (
        d_hat - jnp.mean(d_hat, axis=1, keepdims=True) - hat * jnp.mean(d_hat * hat, axis=1, keepdims=True)
    )
    dr_ref[...] = d_resid
    low = d_resid.astype(BF)
    part_ref[0] += tn(mixed[:, :own], low)
    dm_ref[...] = nt(low, wo_ref[...]).astype(BF)
    for at, v in enumerate((grad, d_normed * hat, d_normed, low.astype(F32), d_pre.astype(F32))):
        vec[at] += fold8(v)

    @pl.when(i == pl.num_programs(0) - 1)
    def _():
        small_ref[...] = jnp.zeros_like(small_ref)
        for at, row in enumerate((0, 1, 2, 3, OWN_ROW)):
            small_ref[row : row + 1] = jnp.sum(vec[at], axis=0, keepdims=True)


def middle(own, mixed, x, cot, valid, wo, w1, w2, bo, g2, c2, b1, b2):
    tokens, width = x.shape
    inner, hidden = wo.shape[0], w1.shape[0]
    n = tokens // BLK
    return pl.pallas_call(
        functools.partial(middle_kernel, own),
        grid=(n,),
        in_specs=[rows(inner), rows(width), rows(width), pl.BlockSpec((1, 1, BLK), lambda i: (i, 0, 0))]
        + [whole((inner, width)), whole((hidden, width)), whole((hidden, width))]
        + [whole((1, width))] * 3
        + [whole((1, hidden)), whole((1, width))],
        out_specs=[
            rows(width),
            rows(width),
            rows(inner),
            held((3, own, width)),
            held((8, width)),
            pl.BlockSpec((1, 8, LANES), lambda i: (i, 0, 0)),
        ],
        out_shape=[
            jax.ShapeDtypeStruct((tokens, width), BF),
            jax.ShapeDtypeStruct((tokens, width), F32),
            jax.ShapeDtypeStruct((tokens, inner), BF),
            jax.ShapeDtypeStruct((3, own, width), F32),
            jax.ShapeDtypeStruct((8, width), F32),
            jax.ShapeDtypeStruct((n, 8, LANES), F32),
        ],
        scratch_shapes=[pltpu.VMEM((5, 8, width), F32)],
        compiler_params=params(1),
        cost_estimate=pl.CostEstimate(
            flops=2 * tokens * width * (6 * width + 3 * own),
            bytes_accessed=14 * tokens * width + 6 * width * width,
            transcendentals=2 * tokens * hidden,
        ),
        name="middle",
    )(mixed, x, cot, valid.astype(F32).reshape(n, 1, BLK), wo, w1, w2, bo, g2, c2, b1, b2)


def finish_kernel(
    bits, own, steps, dq_ref, dk_ref, dv_ref, x_ref, dr_ref, g_ref, wq_ref, wk_ref, wv_ref, mq_ref, mk_ref, mv_ref, n_ref, in_ref,
    dx_ref, gq_ref, gk_ref, gv_ref, small_ref, vec, part, *refs,
):
    step = pl.program_id(0)
    grads = (mq_ref, mk_ref, mv_ref)
    count = len(grads)
    half = part.shape[2] // 2

    def publish(m, total):
        (gq_ref, gk_ref, gv_ref)[m][...] = total.T

    if bits is not None:
        place = Place(bits)
        work = Reduce(place, part, refs[:-3], publish)
        box, *sems = refs[-3:]

    @pl.when(step == 0)
    def _():
        vec[...] = jnp.zeros_like(vec)
        small_ref[...] = in_ref[...]
        if bits is not None:
            greet(place.plane())

    def weight_grad(m):
        mine = grads[m][:, :own]
        part[m] = tn(mine, n_ref[...])
        if m != 1:
            at = 0 if m == 0 else half
            small_ref[OWN_ROW + 1 : OWN_ROW + 2, at : at + own] = jnp.sum(mine.astype(F32), axis=0, keepdims=True)

    for m in range(count):
        pl.when(step == m)(functools.partial(weight_grad, m))

    @pl.when(step >= count)
    def _():
        d_normed = nn(dq_ref[...], wq_ref[...]) + nn(dk_ref[...], wk_ref[...]) + nn(dv_ref[...], wv_ref[...])
        hat, inv = normalize(x_ref[...].astype(F32))
        d_hat = d_normed * g_ref[...]
        dx_ref[...] = dr_ref[...] + inv * (
            d_hat - jnp.mean(d_hat, axis=1, keepdims=True) - hat * jnp.mean(d_hat * hat, axis=1, keepdims=True)
        )
        vec[0] += fold8(d_normed * hat)
        vec[1] += fold8(d_normed)

    if bits is not None:
        for t in range(work.ticks):
            pl.when(step == min(t, steps - 1))(functools.partial(work.tick, t))

    @pl.when(step == steps - 1)
    def _():
        for at in range(2):
            small_ref[4 + at : 5 + at] = jnp.sum(vec[at], axis=0, keepdims=True)
        if bits is None:
            for m in range(count):
                publish(m, part[m])
        else:
            copies = [send(small_ref, box.at[place.d], sems, i, peer) for i, peer in enumerate(place.plane())]
            for one in copies:
                one.start()
            box[place.d] = small_ref[...]
            for one in copies:
                one.wait_recv()
            for one in copies:
                one.wait_send()
            total = box[0]
            for i in range(1, 8):
                total = total + box[i]
            small_ref[...] = total
            work.end()


def finish(dq, dk, dv, x, d_resid, g1, wq, wk, wv, normed1, small, own, bits):
    tokens, width = x.shape
    inner = wq.shape[0]
    hosted = bits is not None
    count = 3
    pad = -(-own // LANES) * LANES
    mine = pl.BlockSpec((tokens, pad), lambda i: (0, 0), pipeline_mode=pl.Buffered(1))

    def late(size):
        return pl.BlockSpec((BLK, size), lambda i: (jnp.maximum(i - count, 0), 0))

    return pl.pallas_call(
        functools.partial(finish_kernel, bits, own, count + tokens // BLK),
        grid=(count + tokens // BLK,),
        in_specs=[late(inner)] * 3
        + [late(width), late(width), whole((1, width))]
        + [whole((inner, width))] * 3
        + [mine] * 3
        + [whole((tokens, width)), whole((8, width))],
        out_specs=[late(width)] + [held((width, own))] * 3 + [held((8, width))],
        out_shape=[jax.ShapeDtypeStruct((tokens, width), F32)]
        + [jax.ShapeDtypeStruct((width, own), F32)] * 3
        + [jax.ShapeDtypeStruct((8, width), F32)],
        scratch_shapes=[pltpu.VMEM((2, 8, width), F32), pltpu.VMEM((count, own, width), F32)]
        + (
            reduce_scratch(count, own, width)
            + [pltpu.VMEM((8, 8, width), F32), pltpu.SemaphoreType.DMA((7,)), pltpu.SemaphoreType.DMA((7,))]
            if hosted
            else []
        ),
        compiler_params=hosting(1, 4) if hosted else params(1),
        cost_estimate=pl.CostEstimate(
            flops=6 * tokens * width * inner, bytes_accessed=16 * tokens * width + 6 * width * inner, transcendentals=0
        ),
        name="finish",
    )(dq, dk, dv, x, d_resid, g1, wq, wk, wv, dq, dk, dv, normed1, small)


def shards(dp, tp, x, g1, c1, wq, bq, wk, wv, bv, wo, bo, g2, c2, w1, b1, w2, b2, seg, valid, cot):
    tokens, width = x.shape
    seqs, length = seg.shape
    own = wq.shape[1]
    bits = bits_of(dp) if dp == 8 else None

    def line(t):
        return t.reshape(1, -1)

    bias = jnp.zeros((8, -(-own // LANES) * LANES), F32).at[:3, :own].set(jnp.stack([bq, bv, b1]))
    fq, fk, fv, biases = gather([wq.T, wk.T, wv.T], bias, dp, tp)
    abq, abv, ab1 = (line(biases[:, r, :own]) for r in range(3))

    normed1, q, k, v, fo = project(x, line(g1), line(c1), fq, fk, fv, abq, abv, [wo], dp, tp)
    mixed, lse, f1, f2 = attend(q, k, v, seg, [w1.T, w2], dp, tp)
    y, d_resid, d_mixed, parts, small, sq = middle(
        own, mixed, x, cot, valid, fo, f1, f2, line(bo), line(g2), line(c2), ab1, line(b2)
    )
    dq, dk, dv, gwo, gw1, gw2 = attend_back(q, k, v, seg, mixed, d_mixed, lse, parts, bits)
    grad_input, gq, gk, gv, small = finish(dq, dk, dv, x, d_resid, line(g1), fq, fk, fv, normed1, small, own, bits)
    if bits is None:
        gwo, gw1, gw2, gq, gk, gv, small = lax.psum((gwo, gw1, gw2, gq, gk, gv, small), "dp")

    weight = valid.astype(F32)
    counted = jnp.maximum(jnp.sum(weight, axis=1), 1.0) * width
    stat = jnp.sum(sq[:, 0, :3].reshape(seqs, length // BLK, 3), axis=1)
    rms = jnp.sqrt(stat / counted[:, None])

    gb2, gg2, gc2, gbo, gg1, gc1 = (small[r] for r in range(6))
    gb1 = small[OWN_ROW, :own]
    gbq = small[OWN_ROW + 1, :own]
    gbv = small[OWN_ROW + 1, width // 2 : width // 2 + own]
    return (y, grad_input, gg1, gc1, gq, gbq, gk, gv, gbv, gwo, gbo, gg2, gc2, gw1, gb1, gw2, gb2, rms)


def solution(mesh):
    dp, tp = mesh.shape["dp"], mesh.shape["tensor"]
    tok, col, row, vec, rep = P("dp", None), P(None, "tensor"), P("tensor", None), P("tensor"), P()
    return jax.shard_map(
        functools.partial(shards, dp, tp),
        mesh=mesh,
        in_specs=(tok, rep, rep, col, vec, col, col, vec, row, rep, rep, rep, col, vec, row, rep, tok, tok, tok),
        out_specs=(tok, tok, rep, rep, col, vec, col, col, vec, row, rep, rep, rep, col, vec, row, rep, tok),
        check_vma=False,
    )
```

time: 672 us -> 468 us (0.70)
  waiting for transfers between devices: 324 us -> 0 us
  Pallas kernels: 230 us -> 422 us
  blocking collectives: 29.9 us -> 0 us
  other arithmetic: 24.3 us -> 4.08 us
  matrix products: 16.8 us -> 0 us
  between operations: 14 us -> 1.1 us
    all_gather x2 -> x0, waiting for transfers between devices: 246 us -> none  [gather(): full = lax.all_gather(mine, ('tensor', 'dp'))]
    pallas_call x6 -> x5, Pallas kernels: 163 us -> 353 us  [the longest x1 88.8 us: gather(): pl.pallas_call(functools.partial(gather_kernel, bits, chunks_of(count, tp...]
    psum x1 -> x0, waiting for transfers between devices: 77.9 us -> none  [shards(): mats = lax.psum((gq, gk, gv), 'dp')]
    psum x1 -> x0, blocking collectives: 29.9 us -> none  [shards(): lax.psum((vec[0], vec[1, :own], vec[2], vec[3], vec[4], last[0], last[1],...]
    dot_general x3 -> x0, matrix products: 16.8 us -> none  [tn(): lax.dot_general(a, b, (((0,), (0,)), ((), ())), preferred_element_type=F32)]
    concatenate x4 -> x0, other arithmetic: 16.6 us -> none  [the longest x1 14.8 us: gather(): twice = jnp.concatenate([full, full], axis=0)]
    unnamed x41 -> x33, local copies, waits for them, and re-layouts: 11.9 us -> 22.9 us
    slice x7 -> x3, local copies, waits for them, and re-layouts: 12 us -> 2.26 us  [the longest x1 0.97 us: shards(): abq, abv, ab1 = (line(biases[:, r, :own]) for r in range(3))]
  transfers between devices with their start and end apart: 3 -> 0, of which waited for: 3 -> 0; matrix products, arithmetic and copies ran while one was open for 2% -> 0% of each run, Pallas kernels for 7% -> 0%
where the time goes in v3:
time: 468 us; the launch traced here: 464 us
  Pallas kernels  422 us (90%)
  local copies, waits for them, and re-layouts  36.7 us (8%)
    pallas_call x1, Pallas kernels, gather(): pl.pallas_call(functools.partial(gather_kernel, bits, chunks_of(count, tp...  88.8 us
    pallas_call x1, Pallas kernels, finish(): pl.pallas_call(functools.partial(finish_kernel, bits, own, count + tokens...  76.1 us
    pallas_call x1, Pallas kernels, attend(): pl.pallas_call(functools.partial(attend_kernel, bits, seqs * n, chunks_of...  73.2 us
    pallas_call x1, Pallas kernels, middle(): pl.pallas_call(functools.partial(middle_kernel, own), grid=(n,), in_specs...  69.4 us
    pallas_call x1, Pallas kernels, attend_back(): pl.pallas_call(functools.partial(attend_back_kernel, seqs * n, bits), gri...  66.6 us
    pallas_call x1, Pallas kernels, project(): pl.pallas_call(functools.partial(project_kernel, bits, steps, chunks_of(c...  48.5 us
    unnamed x33, local copies, waits for them, and re-layouts  22.9 us

profile of v3, /device:TPU:0, one launch (start us, length us, event | category | flops | bytes accessed | tf_op | source)
XLA Modules:
  0.0 464.4 jit_solution(1058617670606562770)
XLA Ops:
  0.7 1.0 constant_dynamic-slice_fusion.1
  1.7 1.0 constant_dynamic-slice_fusion.3
  2.7 0.9 maximum_convert_fusion.mine
  3.6 0.7 stack.30
  4.2 0.7 stack.31
  4.9 0.7 stack.32
  6.2 88.8 %gather_weights.1 = (bf16[1280,1280]{1,0:T(8,128)(2,1)}, bf16[1280,1280]{1,0:T(8,128)(2,1)}, bf16[1280,1280]{1,0:T(8,128)(2,1)}, f32[4,8,384]{2,1,0:T(8,128)}) custom-call(f32[3,40,1280]{2,1,0:T(8,128)} %maximum_convert_fusion.mine, bf16[320,1280]{1,0:T(8,128)(2,1)} %bitcast.20, bf16[320,1280]{1,0:T(8,128)(2,1)} %bitcast.18, bf16[320,1280]{1,0:T(8,128)(2,1)} %bitcast.16, ...), custom_call_target="tpu_custom_call" | custom-call | bytes 29491200 | tf_op jit(solution)/shard_map/gather_weights/pallas_call | solution.py:354
  95.0 1.0 slice_reduce_fusion
  97.3 1.6 dynamic-slice_convert_fusion
  100.2 48.5 %project.1 = (bf16[2048,1280]{1,0:T(8,128)(2,1)}, bf16[2048,1280]{1,0:T(8,128)(2,1)}, bf16[2048,1280]{1,0:T(8,128)(2,1)}, bf16[2048,1280]{1,0:T(8,128)(2,1)}, bf16[1280,1280]{1,0:T(8,128)(2,1)}) custom-call(bf16[2048,1280]{1,0:T(8,128)(2,1)} %x_ref.5, f32[1,1280]{1,0:T(1,128)} %reshape.115.g_ref, f32[1,1280]{1,0:T(1,128)} %reshape.116.c_ref, ...), custom_call_target="tpu_custom_call" | custom-call | flops 20132659200 | bytes 36044800 | tf_op jit(solution)/shard_map/project/pallas_call | solution.py:398
  148.7 0.8 maximum_convert_fusion.1.mine
  150.1 73.2 %attend.1 = (bf16[2048,1280]{1,0:T(8,128)(2,1)}, f32[2048,128]{1,0:T(8,128)}, bf16[1280,1280]{1,0:T(8,128)(2,1)}, bf16[1280,1280]{1,0:T(8,128)(2,1)}) custom-call(bf16[2048,1280]{1,0:T(8,128)(2,1)} %get-tuple-element.64.q_ref, bf16[2048,1280]{1,0:T(8,128)(2,1)} %get-tuple-element.65.k_ref, bf16[2048,1280]{1,0:T(8,128)(2,1)} %get-tuple-element.66.v_ref, ...), custom_call_target="tpu_custom_call" | custom-call | flops 21474836480 | bytes 20971520 | tf_op jit(solution)/shard_map/attend/pallas_call | solution.py:506
  227.0 69.4 %middle.1 = (bf16[2048,1280]{1,0:T(8,128)(2,1)}, f32[2048,1280]{1,0:T(8,128)}, bf16[2048,1280]{1,0:T(8,128)(2,1)}, f32[3,320,1280]{2,1,0:T(8,128)}, f32[8,1280]{1,0:T(8,128)}, /*index=5*/f32[8,8,128]{2,1,0:T(8,128)}) custom-call(bf16[2048,1280]{1,0:T(8,128)(2,1)} %get-tuple-element.67.m_ref.o_ref, bf16[2048,1280]{1,0:T(8,128)(2,1)} %x_ref.5, ...), custom_call_target="tpu_custom_call" | custom-call | flops 45298483200 | bytes 46530560 | tf_op jit(solution)/shard_map/middle/pallas_call | solution.py:719
  296.4 66.6 %attend_back.1 = (bf16[2048,1280]{1,0:T(8,128)(2,1)}, bf16[2048,1280]{1,0:T(8,128)(2,1)}, bf16[2048,1280]{1,0:T(8,128)(2,1)}, f32[320,1280]{1,0:T(8,128)}, f32[1280,320]{1,0:T(8,128)}, /*index=5*/f32[320,1280]{1,0:T(8,128)}) custom-call(bf16[2048,1280]{1,0:T(8,128)(2,1)} %get-tuple-element.64.q_ref, bf16[2048,1280]{1,0:T(8,128)(2,1)} %get-tuple-element.72.do_ref, ...), custom_call_target="tpu_custom_call" | custom-call | flops 53687091200 | bytes 41943040 | tf_op jit(solution)/shard_map/attend_back/pallas_call | solution.py:627
  363.0 76.1 %finish.1 = (f32[2048,1280]{1,0:T(8,128)}, f32[1280,320]{1,0:T(8,128)}, f32[1280,320]{1,0:T(8,128)}, f32[1280,320]{1,0:T(8,128)}, f32[8,1280]{1,0:T(8,128)}) custom-call(bf16[2048,1280]{1,0:T(8,128)(2,1)} %get-tuple-element.75.dq_ref.mq_ref, bf16[2048,1280]{1,0:T(8,128)(2,1)} %get-tuple-element.76.dk_ref.mk_ref, ...), custom_call_target="tpu_custom_call" | custom-call | flops 20132659200 | bytes 51773440 | tf_op jit(solution)/shard_map/finish/pallas_call | solution.py:836
  439.1 2.7 copy.48
  441.8 2.9 copy.49
  444.7 2.7 copy.50
  448.7 1.7 copy.51
  450.4 0.8 slice.71
  452.1 8.9 %copy.58 = f32[2048,1280]{1,0:T(8,128)} copy(f32[2048,1280]{1,0:T(8,128)} %get-tuple-element.181) | data formatting | bytes 20971520
  460.9 1.2 copy.59
  462.1 0.9 copy-done.1
  462.9 1.2 copy.60
  (44 shorter events, 9.7 us)
Async XLA Ops:
  0.7 98.3 %copy-start.6 = (f32[1280]{0:T(1024)S(1)}, f32[1280]{0:T(1024)}, u32[]{:S(2)}) copy-start(f32[1280]{0:T(1024)} %param.22) | copy-start | bytes 15364
  0.7 98.9 %copy-start.7 = (f32[1280]{0:T(1024)S(1)}, f32[1280]{0:T(1024)}, u32[]{:S(2)}) copy-start(f32[1280]{0:T(1024)} %param.23) | copy-start | bytes 15364
  100.2 49.3 %copy-start.5 = (s32[2,1024]{1,0:T(2,128)S(1)}, s32[2,1024]{1,0:T(2,128)}, u32[]{:S(2)}) copy-start(s32[2,1024]{1,0:T(2,128)} %param.37) | copy-start | bytes 24580
  150.1 73.9 %copy-start.3 = (s32[2,1024]{1,0:T(2,128)S(1)}, s32[2,1024]{1,0:T(2,128)}, u32[]{:S(2)}) copy-start(s32[2,1024]{1,0:T(2,128)} %param.38) | copy-start | bytes 24580
  150.1 74.6 %copy-start.8 = (f32[1280]{0:T(1024)S(1)}, f32[1280]{0:T(1024)}, u32[]{:S(2)}) copy-start(f32[1280]{0:T(1024)} %param.30) | copy-start | bytes 15364
  150.1 75.2 %copy-start.9 = (f32[1280]{0:T(1024)S(1)}, f32[1280]{0:T(1024)}, u32[]{:S(2)}) copy-start(f32[1280]{0:T(1024)} %param.31) | copy-start | bytes 15364
  150.1 75.8 %copy-start.10 = (f32[1280]{0:T(1024)S(1)}, f32[1280]{0:T(1024)}, u32[]{:S(2)}) copy-start(f32[1280]{0:T(1024)} %param.32) | copy-start | bytes 15364
  150.1 76.4 %copy-start.11 = (f32[1280]{0:T(1024)S(1)}, f32[1280]{0:T(1024)}, u32[]{:S(2)}) copy-start(f32[1280]{0:T(1024)} %param.36) | copy-start | bytes 15364
  441.8 5.6 %copy-start.4 = (f32[8,1280]{1,0:T(8,128)S(1)}, f32[8,1280]{1,0:T(8,128)}, u32[]{:S(2)}) copy-start(f32[8,1280]{1,0:T(8,128)} %get-tuple-element.82) | copy-start | bytes 122884
  441.8 6.9 %copy-start = (f32[1280,320]{1,0:T(8,128)S(1)}, f32[1280,320]{1,0:T(8,128)}, u32[]{:S(2)}) copy-start(f32[1280,320]{1,0:T(8,128)} %get-tuple-element.139) | copy-start | bytes 4915204
  452.1 8.9 %copy-start.2 = (f32[320,1280]{1,0:T(8,128)S(1)}, f32[320,1280]{1,0:T(8,128)}, u32[]{:S(2)}) copy-start(f32[320,1280]{1,0:T(8,128)} %get-tuple-element.189) | copy-start | bytes 4915204
  460.9 2.0 copy-start.1
